TPU v7x, 32 devices: a whole 2x2x4 slice. The times are simulated.
32 devices in a mesh: dp: 8 (over z, core), tensor: 4 (over y, x).
Axes of the slice: x: 2, y: 2, z: 4, core: 2. Of those that a mesh axis runs over, the one named last changes fastest.
Arguments:
- hidden_in: bfloat16 [32, 1024, 2048], P('dp', 'tensor'), may hold values from -6 to 6
- cotangent: bfloat16 [32, 1024, 2048], P('dp', 'tensor'), may hold values from -6 to 6
- lengths: int32 [32], P('dp'), may hold values from 256 to 1024, as said below
- adapter_ids: int32 [32], P('dp'), may hold values from 0 to 7
- attn_norm: bfloat16 [2048], replicated, may hold values from 0.5 to 1.5
- q_norm: bfloat16 [128], replicated, may hold values from 0.5 to 1.5
- k_norm: bfloat16 [128], replicated, may hold values from 0.5 to 1.5
- ffn_norm: bfloat16 [2048], replicated, may hold values from 0.5 to 1.5
- w_q: bfloat16 [2048, 2048], P(None, 'tensor'), may hold values from -0.125 to 0.125
- key_weight: bfloat16 [2048, 1024], P(None, 'tensor'), may hold values from -0.125 to 0.125
- value_weight: bfloat16 [2048, 1024], P(None, 'tensor'), may hold values from -0.125 to 0.125
- w_o: bfloat16 [2048, 2048], P('tensor'), may hold values from -0.5 to 0.5
- w_gate: bfloat16 [6144, 2048], P('tensor'), may hold values from -0.125 to 0.125
- w_up: bfloat16 [6144, 2048], P('tensor'), may hold values from -0.125 to 0.125
- w_down: bfloat16 [6144, 2048], P('tensor'), may hold values from -0.15625 to 0.15625
- a_q: bfloat16 [8, 2048, 16], replicated, may hold values from -0.125 to 0.125
- b_q: bfloat16 [8, 16, 2048], P(None, None, 'tensor'), may hold values from -0.75 to 0.75
- a_k: bfloat16 [8, 2048, 16], replicated, may hold values from -0.125 to 0.125
- key_second_factor: bfloat16 [8, 16, 1024], P(None, None, 'tensor'), may hold values from -0.75 to 0.75
- a_v: bfloat16 [8, 2048, 16], replicated, may hold values from -0.125 to 0.125
- value_second_factor: bfloat16 [8, 16, 1024], P(None, None, 'tensor'), may hold values from -0.75 to 0.75
- a_o: bfloat16 [8, 2048, 16], P(None, 'tensor'), may hold values from -0.5 to 0.5
- b_o: bfloat16 [8, 16, 2048], replicated, may hold values from -0.75 to 0.75
- a_gate: bfloat16 [8, 2048, 16], replicated, may hold values from -0.125 to 0.125
- b_gate: bfloat16 [6144, 8, 16], P('tensor'), may hold values from -0.75 to 0.75
- a_up: bfloat16 [8, 2048, 16], replicated, may hold values from -0.125 to 0.125
- b_up: bfloat16 [6144, 8, 16], P('tensor'), may hold values from -0.75 to 0.75
- a_down: bfloat16 [6144, 8, 16], P('tensor'), may hold values from -0.15625 to 0.15625
- b_down: bfloat16 [8, 16, 2048], replicated, may hold values from -0.75 to 0.75
Outputs:
- output: bfloat16 [32, 1024, 2048], P('dp', 'tensor')
- d_input: bfloat16 [32, 1024, 2048], P('dp', 'tensor')
- g_a_q: float32 [8, 2048, 16], replicated
- g_b_q: float32 [8, 16, 2048], P(None, None, 'tensor')
- g_a_k: float32 [8, 2048, 16], replicated
- g_b_k: float32 [8, 16, 1024], P(None, None, 'tensor')
- g_a_v: float32 [8, 2048, 16], replicated
- g_b_v: float32 [8, 16, 1024], P(None, None, 'tensor')
- g_a_o: float32 [8, 2048, 16], P(None, 'tensor')
- g_b_o: float32 [8, 16, 2048], replicated
- g_a_gate: float32 [8, 2048, 16], replicated
- g_b_gate: float32 [6144, 8, 16], P('tensor')
- g_a_up: float32 [8, 2048, 16], replicated
- g_b_up: float32 [6144, 8, 16], P('tensor')
- g_a_down: float32 [6144, 8, 16], P('tensor')
- g_b_down: float32 [8, 16, 2048], replicated
Inputs may be any that keep to these rules, and one draw needn't show every extreme that they name: `lengths`: every row holds between 256 and 1024 valid tokens; some row holds exactly 1024 and some exactly 256.
All inputs are finite; a program needn't handle non-finite values.
Results may differ from a plain program's by a relative error of at most 0.02.
Values may be sent and summed in bfloat16 or wider, within the bound.
No kernel may reach another device: no remote copies, remote signals or barrier semaphores. Data moves between devices by JAX's collectives and lax.ppermute only.
A program may use at most 384 MiB of HBM per device.

v0:
```python
import jax
import jax.numpy as jnp
from jax import lax
from jax.sharding import PartitionSpec as P

epsilon = 1e-06
rope_base = 1000000.0
highest = lax.Precision.HIGHEST


def normed(values, gain):
    return values * lax.rsqrt(jnp.mean(values * values, axis=-1, keepdims=True) + epsilon) * gain


def rope_tables(slot_count, head_dim):
    position = jnp.arange(slot_count).astype(jnp.float32)
    exponent = jnp.arange(head_dim // 2).astype(jnp.float32) * (2.0 / head_dim)
    angles = position[:, None] * (rope_base ** (-exponent))[None, :]
    cosine = jnp.cos(angles)
    sine = jnp.sin(angles)
    return (jnp.concatenate([cosine, cosine], -1), jnp.concatenate([sine, sine], -1))


def rotate(values, cosine, sine):
    half_dim = values.shape[-1] // 2
    turned = jnp.concatenate([-values[..., half_dim:], values[..., :half_dim]], -1)
    return values * cosine[:, None, :] + turned * sine[:, None, :]


def head_prep(raw, gain, cosine, sine):
    head_dim = gain.shape[0]
    shaped = raw.reshape(raw.shape[:-1] + (raw.shape[-1] // head_dim, head_dim))
    return rotate(normed(shaped, gain), cosine, sine)


def allowed_pairs(slot_count, length):
    position = jnp.arange(slot_count)
    return (position[None, :] <= position[:, None]) & (position[None, :] < length)


def masked_scores(grouped, key_rows, length):
    slot_count, kv_heads, head_dim = key_rows.shape
    scores = jnp.einsum(
        "qkgd,tkd->kgqt", grouped, key_rows, preferred_element_type=jnp.float32
    ) * head_dim ** (-0.5)
    return jnp.where(allowed_pairs(slot_count, length), scores, -1e30)


def attend(queries, key_rows, value_row_block, length):
    slot_count, kv_heads, head_dim = key_rows.shape
    grouped = queries.reshape(slot_count, kv_heads, -1, head_dim)
    scores = masked_scores(grouped, key_rows, length)
    row_max = jnp.max(scores, axis=-1, keepdims=True)
    exp_terms = jnp.exp(scores - row_max)
    row_total = jnp.sum(exp_terms, axis=-1, keepdims=True)
    probabilities = (exp_terms / row_total).astype(jnp.bfloat16)
    attended = jnp.einsum(
        "kgqt,tkd->qkgd", probabilities, value_row_block, preferred_element_type=jnp.float32
    )
    return (
        attended.reshape(slot_count, -1).astype(jnp.bfloat16),
        (row_max + jnp.log(row_total))[..., 0],
    )


def attend_back(queries, key_rows, value_row_block, length, log_total, d_attended):
    slot_count, kv_heads, head_dim = key_rows.shape
    scale = head_dim ** (-0.5)
    grouped = queries.reshape(slot_count, kv_heads, -1, head_dim)
    scores = masked_scores(grouped, key_rows, length)
    probabilities = jnp.exp(scores - log_total[..., None])
    d_grouped = d_attended.reshape(slot_count, kv_heads, -1, head_dim)
    d_probs = jnp.einsum(
        "qkgd,tkd->kgqt", d_grouped, value_row_block, preferred_element_type=jnp.float32
    )
    inner = jnp.sum(probabilities * d_probs, axis=-1, keepdims=True)
    d_scores = (probabilities * (d_probs - inner)).astype(jnp.bfloat16)
    d_queries = (
        jnp.einsum("kgqt,tkd->qkgd", d_scores, key_rows, preferred_element_type=jnp.float32) * scale
    )
    d_keys = (
        jnp.einsum("kgqt,qkgd->tkd", d_scores, grouped, preferred_element_type=jnp.float32) * scale
    )
    d_values = jnp.einsum(
        "kgqt,qkgd->tkd",
        probabilities.astype(jnp.bfloat16),
        d_grouped,
        preferred_element_type=jnp.float32,
    )
    return (d_queries.reshape(slot_count, -1, head_dim), d_keys, d_values)


def local(
    hidden_in,
    cotangent,
    lengths,
    adapter_ids,
    attn_norm,
    q_norm,
    k_norm,
    ffn_norm,
    w_q,
    key_weight,
    value_weight,
    w_o,
    w_gate,
    w_up,
    w_down,
    a_q,
    b_q,
    a_k,
    key_second_factor,
    a_v,
    value_second_factor,
    a_o,
    b_o,
    a_gate,
    b_gate,
    a_up,
    b_up,
    a_down,
    b_down,
):
    row_count, shard_len, width = hidden_in.shape
    tensor_size = lax.axis_size("tensor")
    slot_count = shard_len * tensor_size
    offset = lax.axis_index("tensor") * shard_len
    head_dim = q_norm.shape[0]
    rank = a_q.shape[2]
    adapter_count = a_q.shape[0]
    slot_local = offset + jnp.arange(shard_len)
    valid = (slot_local[None, :] < lengths[:, None]).astype(jnp.float32)
    onehot = (adapter_ids[:, None] == jnp.arange(adapter_count)[None, :]).astype(jnp.float32)
    cosine, sine = rope_tables(slot_count, head_dim)
    attn_gain = attn_norm.astype(jnp.float32)
    ffn_gain = ffn_norm.astype(jnp.float32)
    q_gain = q_norm.astype(jnp.float32)
    k_gain = k_norm.astype(jnp.float32)

    def pick(table):
        return jnp.take(table, adapter_ids, axis=0)

    def pick_mid(table):
        return jnp.take(table, adapter_ids, axis=1)

    def spread(per_row):
        return jnp.einsum("ra,rxy->axy", onehot, per_row, precision=highest)

    def spread_mid(per_row):
        return jnp.einsum("ra,fry->fay", onehot, per_row, precision=highest)

    hidden32 = hidden_in.astype(jnp.float32)
    xn_local = normed(hidden32, attn_gain).astype(jnp.bfloat16)
    xn_full = lax.all_gather(xn_local, "tensor", axis=1, tiled=True)
    a_qkv = jnp.concatenate([pick(a_q), pick(a_k), pick(a_v)], -1)
    h_qkv = jnp.einsum("rsd,rdk->rsk", xn_full, a_qkv, preferred_element_type=jnp.float32).astype(
        jnp.bfloat16
    )
    h_q = h_qkv[..., :rank]
    h_k = h_qkv[..., rank : 2 * rank]
    h_v = h_qkv[..., 2 * rank :]

    def project(weight, low_rank, table):
        main_part = jnp.einsum("rsd,do->rso", xn_full, weight, preferred_element_type=jnp.float32)
        return main_part + jnp.einsum(
            "rsk,rko->rso", low_rank, pick(table), preferred_element_type=jnp.float32
        )

    q_raw = project(w_q, h_q, b_q)
    k_raw = project(key_weight, h_k, key_second_factor)
    v_raw = project(value_weight, h_v, value_second_factor)
    q_rot = head_prep(q_raw, q_gain, cosine, sine).astype(jnp.bfloat16)
    k_rot = head_prep(k_raw, k_gain, cosine, sine).astype(jnp.bfloat16)
    value_row_block = v_raw.astype(jnp.bfloat16).reshape(k_rot.shape)
    attn_cat, log_total = lax.map(
        lambda record: attend(*record), (q_rot, k_rot, value_row_block, lengths)
    )
    out_part = jnp.einsum("rso,od->rsd", attn_cat, w_o, preferred_element_type=jnp.float32)
    h_o_part = jnp.einsum("rso,rok->rsk", attn_cat, pick(a_o), preferred_element_type=jnp.float32)
    out_shard, h_o_shard = (
        lax.psum_scatter(out_part, "tensor", scatter_dimension=1, tiled=True),
        lax.psum_scatter(h_o_part, "tensor", scatter_dimension=1, tiled=True),
    )
    b_o_rows = pick(b_o)
    attn_out = out_shard + jnp.einsum(
        "rsk,rkd->rsd", h_o_shard, b_o_rows.astype(jnp.float32), precision=highest
    )
    residual = hidden32 + attn_out
    x2_local = normed(residual, ffn_gain).astype(jnp.bfloat16)
    a_gu = jnp.concatenate([pick(a_gate), pick(a_up)], -1)
    gate_w, up_w, down_w, gate_b, up_b, down_a = (w_gate, w_up, w_down, b_gate, b_up, a_down)
    ffn_rows = lax.all_gather(x2_local, "tensor", axis=1, tiled=True)
    h_gu = jnp.einsum("rsd,rdk->rsk", ffn_rows, a_gu, preferred_element_type=jnp.float32).astype(
        jnp.bfloat16
    )
    h_gate = h_gu[..., :rank]
    h_up = h_gu[..., rank:]
    gate_b_rows = pick_mid(gate_b)
    up_b_rows = pick_mid(up_b)
    down_a_rows = pick_mid(down_a)
    gate_pre = jnp.einsum(
        "rsd,fd->rsf", ffn_rows, gate_w, preferred_element_type=jnp.float32
    ) + jnp.einsum("rsk,frk->rsf", h_gate, gate_b_rows, preferred_element_type=jnp.float32)
    up_pre = jnp.einsum(
        "rsd,fd->rsf", ffn_rows, up_w, preferred_element_type=jnp.float32
    ) + jnp.einsum("rsk,frk->rsf", h_up, up_b_rows, preferred_element_type=jnp.float32)
    sigmoid_gate = jax.nn.sigmoid(gate_pre)
    silu_gate = gate_pre * sigmoid_gate
    hidden_act = (silu_gate * up_pre).astype(jnp.bfloat16)
    down_part = jnp.einsum("rsf,fd->rsd", hidden_act, down_w, preferred_element_type=jnp.float32)
    h_down_part = jnp.einsum(
        "rsf,frk->rsk", hidden_act, down_a_rows, preferred_element_type=jnp.float32
    )
    ffn_shard, h_down = (
        lax.psum_scatter(
            down_part.astype(jnp.bfloat16), "tensor", scatter_dimension=1, tiled=True
        ).astype(jnp.float32),
        lax.psum_scatter(
            h_down_part.astype(jnp.bfloat16), "tensor", scatter_dimension=1, tiled=True
        ).astype(jnp.float32),
    )
    b_down_rows = pick(b_down)
    ffn_out = ffn_shard + jnp.einsum(
        "rsk,rkd->rsd", h_down, b_down_rows.astype(jnp.float32), precision=highest
    )
    output = ((residual + ffn_out) * valid[..., None]).astype(jnp.bfloat16)
    d_out = cotangent.astype(jnp.float32) * valid[..., None]
    d_ffn = d_out.astype(jnp.bfloat16)
    dh_down = jnp.einsum(
        "rsd,rkd->rsk", d_ffn, b_down_rows, preferred_element_type=jnp.float32
    ).astype(jnp.bfloat16)
    grad_b_down = spread(
        jnp.einsum("rsk,rsd->rkd", h_down, d_ffn.astype(jnp.float32), precision=highest)
    )
    d_ffn_rows, dh_down_rows = (
        lax.all_gather(d_ffn, "tensor", axis=1, tiled=True),
        lax.all_gather(dh_down, "tensor", axis=1, tiled=True),
    )
    d_act = jnp.einsum(
        "rsd,fd->rsf", d_ffn_rows, down_w, preferred_element_type=jnp.float32
    ) + jnp.einsum("rsk,frk->rsf", dh_down_rows, down_a_rows, preferred_element_type=jnp.float32)
    grad_down_a = spread_mid(
        jnp.einsum("rsf,rsk->frk", hidden_act, dh_down_rows, preferred_element_type=jnp.float32)
    )
    d_gate = (d_act * up_pre * sigmoid_gate * (1.0 + gate_pre * (1.0 - sigmoid_gate))).astype(
        jnp.bfloat16
    )
    d_up = (d_act * silu_gate).astype(jnp.bfloat16)
    d_rows = jnp.einsum(
        "rsf,fd->rsd", d_gate, gate_w, preferred_element_type=jnp.float32
    ) + jnp.einsum("rsf,fd->rsd", d_up, up_w, preferred_element_type=jnp.float32)
    dh_gate_part = jnp.einsum(
        "rsf,frk->rsk", d_gate, gate_b_rows, preferred_element_type=jnp.float32
    )
    dh_up_part = jnp.einsum("rsf,frk->rsk", d_up, up_b_rows, preferred_element_type=jnp.float32)
    dh_gu_part = jnp.concatenate([dh_gate_part, dh_up_part], -1)
    grad_gate_b = spread_mid(
        jnp.einsum("rsk,rsf->frk", h_gate, d_gate, preferred_element_type=jnp.float32)
    )
    grad_up_b = spread_mid(
        jnp.einsum("rsk,rsf->frk", h_up, d_up, preferred_element_type=jnp.float32)
    )
    d_x2, dh_gu = (
        lax.psum_scatter(d_rows, "tensor", scatter_dimension=1, tiled=True),
        lax.psum_scatter(dh_gu_part, "tensor", scatter_dimension=1, tiled=True),
    )
    grad_b_gate, grad_b_up, grad_a_down = (grad_gate_b, grad_up_b, grad_down_a)
    dh_gu_low = dh_gu.astype(jnp.bfloat16)
    d_x2 = d_x2 + jnp.einsum("rsk,rdk->rsd", dh_gu_low, a_gu, preferred_element_type=jnp.float32)
    grad_a_gu = spread(
        jnp.einsum("rsd,rsk->rdk", x2_local, dh_gu_low, preferred_element_type=jnp.float32)
    )
    grad_a_gate = grad_a_gu[..., :rank]
    grad_a_up = grad_a_gu[..., rank:]
    ffn_pull = jax.vjp(lambda values: normed(values, ffn_gain), residual)[1]
    d_residual = d_out + ffn_pull(d_x2)[0]
    d_attn = d_residual.astype(jnp.bfloat16)
    dh_o = jnp.einsum("rsd,rkd->rsk", d_attn, b_o_rows, preferred_element_type=jnp.float32).astype(
        jnp.bfloat16
    )
    grad_b_o = spread(
        jnp.einsum("rsk,rsd->rkd", h_o_shard, d_attn.astype(jnp.float32), precision=highest)
    )
    d_attn_full, dh_o_full = (
        lax.all_gather(d_attn, "tensor", axis=1, tiled=True),
        lax.all_gather(dh_o, "tensor", axis=1, tiled=True),
    )
    a_o_rows = pick(a_o)
    d_cat = jnp.einsum(
        "rsd,od->rso", d_attn_full, w_o, preferred_element_type=jnp.float32
    ) + jnp.einsum("rsk,rok->rso", dh_o_full, a_o_rows, preferred_element_type=jnp.float32)
    d_cat = d_cat.astype(jnp.bfloat16)
    grad_a_o = spread(
        jnp.einsum("rso,rsk->rok", attn_cat, dh_o_full, preferred_element_type=jnp.float32)
    )
    d_qrot, d_krot, d_values = lax.map(
        lambda record: attend_back(*record),
        (q_rot, k_rot, value_row_block, lengths, log_total, d_cat),
    )
    q_pull = jax.vjp(lambda raw: head_prep(raw, q_gain, cosine, sine), q_raw)[1]
    k_pull = jax.vjp(lambda raw: head_prep(raw, k_gain, cosine, sine), k_raw)[1]
    d_q = q_pull(d_qrot)[0].astype(jnp.bfloat16)
    d_k = k_pull(d_krot)[0].astype(jnp.bfloat16)
    d_v = d_values.reshape(v_raw.shape).astype(jnp.bfloat16)
    d_rows_attn = jnp.einsum("rso,do->rsd", d_q, w_q, preferred_element_type=jnp.float32)
    d_rows_attn = d_rows_attn + jnp.einsum(
        "rso,do->rsd", d_k, key_weight, preferred_element_type=jnp.float32
    )
    d_rows_attn = d_rows_attn + jnp.einsum(
        "rso,do->rsd", d_v, value_weight, preferred_element_type=jnp.float32
    )
    dh_qkv_part = jnp.concatenate(
        [
            jnp.einsum("rso,rko->rsk", d_q, pick(b_q), preferred_element_type=jnp.float32),
            jnp.einsum(
                "rso,rko->rsk", d_k, pick(key_second_factor), preferred_element_type=jnp.float32
            ),
            jnp.einsum(
                "rso,rko->rsk", d_v, pick(value_second_factor), preferred_element_type=jnp.float32
            ),
        ],
        -1,
    )
    grad_b_q = spread(jnp.einsum("rsk,rso->rko", h_q, d_q, preferred_element_type=jnp.float32))
    grad_b_k = spread(jnp.einsum("rsk,rso->rko", h_k, d_k, preferred_element_type=jnp.float32))
    grad_b_v = spread(jnp.einsum("rsk,rso->rko", h_v, d_v, preferred_element_type=jnp.float32))
    d_xn, dh_qkv = (
        lax.psum_scatter(
            d_rows_attn.astype(jnp.bfloat16), "tensor", scatter_dimension=1, tiled=True
        ).astype(jnp.float32),
        lax.psum_scatter(
            dh_qkv_part.astype(jnp.bfloat16), "tensor", scatter_dimension=1, tiled=True
        ).astype(jnp.float32),
    )
    dh_qkv_low = dh_qkv.astype(jnp.bfloat16)
    d_xn = d_xn + jnp.einsum("rsk,rdk->rsd", dh_qkv_low, a_qkv, preferred_element_type=jnp.float32)
    grad_a_qkv = spread(
        jnp.einsum("rsd,rsk->rdk", xn_local, dh_qkv_low, preferred_element_type=jnp.float32)
    )
    attn_pull = jax.vjp(lambda values: normed(values, attn_gain), hidden32)[1]
    d_input = (d_residual + attn_pull(d_xn)[0]).astype(jnp.bfloat16)
    split_sums = (
        lax.psum(grad_b_q.astype(jnp.bfloat16), "dp").astype(jnp.float32),
        lax.psum(grad_b_k.astype(jnp.bfloat16), "dp").astype(jnp.float32),
        lax.psum(grad_b_v.astype(jnp.bfloat16), "dp").astype(jnp.float32),
        lax.psum(grad_a_o.astype(jnp.bfloat16), "dp").astype(jnp.float32),
        lax.psum(grad_b_gate.astype(jnp.bfloat16), "dp").astype(jnp.float32),
        lax.psum(grad_b_up.astype(jnp.bfloat16), "dp").astype(jnp.float32),
        lax.psum(grad_a_down.astype(jnp.bfloat16), "dp").astype(jnp.float32),
    )
    whole_sums = lax.psum(
        (
            grad_a_qkv[..., :rank],
            grad_a_qkv[..., rank : 2 * rank],
            grad_a_qkv[..., 2 * rank :],
            grad_b_o,
            grad_a_gate,
            grad_a_up,
            grad_b_down,
        ),
        ("dp", "tensor"),
    )
    return (
        output,
        d_input,
        whole_sums[0],
        split_sums[0],
        whole_sums[1],
        split_sums[1],
        whole_sums[2],
        split_sums[2],
        split_sums[3],
        whole_sums[3],
        whole_sums[4],
        split_sums[4],
        whole_sums[5],
        split_sums[5],
        split_sums[6],
        whole_sums[6],
    )


def solution(mesh):
    placed = (
        P("dp", "tensor", None),
        P("dp", "tensor", None),
        P("dp"),
        P("dp"),
        P(),
        P(),
        P(),
        P(),
        P(None, "tensor"),
        P(None, "tensor"),
        P(None, "tensor"),
        P("tensor", None),
        P("tensor", None),
        P("tensor", None),
        P("tensor", None),
        P(),
        P(None, None, "tensor"),
        P(),
        P(None, None, "tensor"),
        P(),
        P(None, None, "tensor"),
        P(None, "tensor", None),
        P(),
        P(),
        P("tensor", None, None),
        P(),
        P("tensor", None, None),
        P("tensor", None, None),
        P(),
    )
    return jax.shard_map(
        local,
        mesh=mesh,
        in_specs=placed,
        out_specs=(
            P("dp", "tensor", None),
            P("dp", "tensor", None),
            P(),
            P(None, None, "tensor"),
            P(),
            P(None, None, "tensor"),
            P(),
            P(None, None, "tensor"),
            P(None, "tensor", None),
            P(),
            P(),
            P("tensor", None, None),
            P(),
            P("tensor", None, None),
            P("tensor", None, None),
            P(),
        ),
        check_vma=False,
    )
```

profile of v0, /device:TPU:0, one launch (start us, length us, event | category | flops | bytes accessed | tf_op | source)
XLA Modules:
  0.0 2512.5 jit_solution(16653419093874698476)
XLA Ops:
  36.4 140.2 %all-gather.5.cloned.1.call-done = bf16[4,1024,2048]{2,1,0:T(8,128)(2,1)} async-done(((bf16[4,256,2048]{2,1,0:T(8,128)(2,1)}), bf16[4,1024,2048]{2,1,0:T(8,128)(2,1)}) %all-gather.5.cloned.1.call-update) | async-done | bytes 16777232 | tf_op jit(solution)/shard_map/all_gather | solution.py:154
  176.7 15.8 fusion.77
  192.5 8.9 convolution_convert_fusion.4
  222.2 12.6 fusion.83
  246.9 12.6 fusion.86
  263.8 76.0 %while.26 = (s32[]{:T(128)}, bf16[4,1024,512]{1,2,0:T(8,128)(2,1)}, f32[4,2,2,1024]{3,2,1,0:T(2,128)}, bf16[4,1024,2,128]{1,3,2,0:T(8,128)(2,1)}, s32[4]{0:T(128...) while((s32[]{:T(128)}, bf16[4,1024,512]{1,2,0:T(8,128)(2,1)}, ...), condition=%wide.region_6.10_spmd, body=%wide.region_3.9_spmd.sunk | while | flops 2200433664 | bytes 62001256 | solution.py:175
  313.3 6.5 fusion.262
  332.3 6.5 fusion.262
  343.5 17.8 fusion.73
  367.9 291.6 %reduce-scatter.9.cloned.1.call-done = f32[4,256,2048]{2,1,0:T(8,128)} async-done(((f32[4,1024,2048]{2,1,0:T(8,128)}), f32[4,256,2048]{2,1,0:T(8,128)}) %reduce-scatter.9.cloned.1.call-update) | async-done | bytes 8388624 | tf_op jit(solution)/shard_map/reduce_scatter | solution.py:181
  659.6 7.9 multiply_reduce_fusion.2
  688.2 11.4 all_gather.21
  700.2 10.7 fusion.101
  710.9 121.1 %all-gather.7.cloned.1.call-done = bf16[4,1024,2048]{2,1,0:T(8,128)(2,1)} async-done(((bf16[4,256,2048]{2,1,0:T(8,128)(2,1)}), bf16[4,1024,2048]{2,1,0:T(8,128)(2,1)}) %all-gather.7.cloned.1.call-update) | async-done | bytes 16777232 | tf_op jit(solution)/shard_map/all_gather | solution.py:192
  832.0 8.6 convolution_convert_fusion.5
  840.6 12.5 fusion.106
  853.1 10.2 fusion.110
  863.3 35.6 %convolution_add_fusion.1 = f32[4,1024,1536]{2,1,0:T(8,128)} fusion(f32[4,1024,1536]{2,1,0:T(8,128)} %fusion.106, bf16[4,1024,2048]{2,1,0:T(8,128)(2,1)} %all-gather.7.cloned.1.call-done, bf16[1536,2048]{1,0:T(8,128)(2,1)} %param.58), kind=kOutput, calls=%fused_computation.81 | convolution fusion | flops 25776095232 | bytes 73400320 | tf_op jit(solution)/shard_map/rsd,fd->rsf/dot_general | solution.py:204
  898.9 37.6 %convolution_add_fusion.2 = f32[4,1024,1536]{2,1,0:T(8,128)} fusion(f32[4,1024,1536]{2,1,0:T(8,128)} %fusion.110, bf16[4,1024,2048]{2,1,0:T(8,128)(2,1)} %all-gather.7.cloned.1.call-done, bf16[1536,2048]{1,0:T(8,128)(2,1)} %param.57), kind=kOutput, calls=%fused_computation.82 | convolution fusion | flops 25776095232 | bytes 73400320 | tf_op jit(solution)/shard_map/rsd,fd->rsf/dot_general | solution.py:201
  936.5 54.5 %all-gather.9.cloned.1.call-done = bf16[4,1024,2048]{2,1,0:T(8,128)(2,1)} async-done(((bf16[4,256,2048]{2,1,0:T(8,128)(2,1)}), bf16[4,1024,2048]{2,1,0:T(8,128)(2,1)}) %all-gather.9.cloned.1.call-update) | async-done | bytes 16777232 | tf_op jit(solution)/shard_map/all_gather | solution.py:236
  991.0 53.3 %multiply_convert_fusion = (bf16[4,1024,1536]{2,1,0:T(8,128)(2,1)}, bf16[4,1024,1536]{2,1,0:T(8,128)(2,1)}, bf16[4,1024,1536]{2,1,0:T(8,128)(2,1)}) fusion(f32[4,1024,1536]{2,1,0:T(8,128)} %convolution_add_fusion.2, f32[4,1024,1536]{2,1,0:T(8,128)} %convolution_add_fusion.1, f32[4,1024,1536]{2,1,0:T(8,128)} %fusion.101, ...), kind=kOutput, calls=%fused_computation.75 | convolution fusion | flops 25870467072 | bytes 136314880 | tf_op jit(solution)/shard_map/rsd,fd->rsf/dot_general | solution.py:239
  1044.4 7.9 fusion.108
  1052.3 33.7 %fusion.62 = f32[4,1024,2048]{2,1,0:T(8,128)} fusion(bf16[4,1024,1536]{2,1,0:T(8,128)(2,1)} %get-tuple-element.238, bf16[1536,2048]{1,0:T(8,128)(2,1)} %param.57), kind=kOutput, calls=%fused_computation.121 | convolution fusion | flops 25769803776 | bytes 52428800 | tf_op jit(solution)/shard_map/rsf,fd->rsd/dot_general | solution.py:249
  1086.0 7.9 fusion.104
  1094.9 38.3 %convolution_add_fusion.3 = f32[4,1024,2048]{2,1,0:T(8,128)} fusion(f32[4,1024,2048]{2,1,0:T(8,128)} %fusion.62, bf16[4,1024,1536]{2,1,0:T(8,128)(2,1)} %get-tuple-element.237, bf16[1536,2048]{1,0:T(8,128)(2,1)} %param.58), kind=kOutput, calls=%fused_computation.83 | convolution fusion | flops 25778192384 | bytes 85983232 | tf_op jit(solution)/shard_map/rsf,fd->rsd/dot_general | solution.py:251
  1133.3 288.6 %reduce-scatter.17.cloned.1.call-done = f32[4,256,2048]{2,1,0:T(8,128)} async-done(((f32[4,1024,2048]{2,1,0:T(8,128)}), f32[4,256,2048]{2,1,0:T(8,128)}) %reduce-scatter.17.cloned.1.call-update) | async-done | bytes 8388624 | tf_op jit(solution)/shard_map/reduce_scatter | solution.py:264
  1421.9 7.6 multiply_reduce_fusion.1
  1439.1 8.6 convolution_convert_fusion.11
  1452.0 11.5 all_gather.23
  1463.5 134.0 %all-gather.11.cloned.1.call-done = bf16[4,1024,2048]{2,1,0:T(8,128)(2,1)} async-done(((bf16[4,256,2048]{2,1,0:T(8,128)(2,1)}), bf16[4,1024,2048]{2,1,0:T(8,128)(2,1)}) %all-gather.11.cloned.1.call-update) | async-done | bytes 16777232 | tf_op jit(solution)/shard_map/all_gather | solution.py:285
  1597.5 12.4 fusion.71
  1613.2 238.1 %while.27 = (s32[]{:T(128)}, f32[4,1024,4,128]{1,3,2,0:T(8,128)}, f32[4,1024,2,128]{1,3,2,0:T(8,128)}, bf16[4,1024,2,128]{1,3,2,0:T(8,128)(2,1)}, bf16[4,1024,2,...) while((s32[]{:T(128)}, f32[4,1024,4,128]{1,3,2,0:T(8,128)}, ...), condition=%wide.region_17.24_spmd, body=%wide.region_15.23_spmd.sunk | while | flops 5434504192 | bytes 163173616 | solution.py:296
  1615.0 9.6 fusion.272
  1631.4 12.5 fusion.274
  1643.9 12.1 fusion.275
  1664.0 9.1 fusion.277
  1674.4 9.6 fusion.272
  1690.9 12.5 fusion.274
  1703.4 12.1 fusion.275
  1723.3 9.1 fusion.277
  1733.8 9.6 fusion.272
  1750.2 12.5 fusion.274
  1762.7 12.1 fusion.275
  1782.7 9.1 fusion.277
  1793.1 9.6 fusion.272
  1809.6 12.5 fusion.274
  1822.1 12.1 fusion.275
  1842.1 9.1 fusion.277
  1862.3 9.4 broadcast_multiply_fusion
  1876.3 8.6 multiply_reduce_fusion
  1884.9 7.8 fusion.48
  1898.3 32.4 %convolution_convert_fusion = bf16[4,1024,2048]{2,1,0:T(8,128)(2,1)} fusion(bf16[4,1024,1536]{2,1,0:T(8,128)(2,1)} %get-tuple-element.239, bf16[1536,2048]{1,0:T(8,128)(2,1)} %param.59), kind=kOutput, calls=%fused_computation.89 | convolution fusion | flops 25778192384 | bytes 35651584 | tf_op jit(solution)/shard_map/rsf,fd->rsd/dot_general | solution.py:210
  1931.7 6.5 fusion.117
  1939.7 6.5 fusion.114
  1976.8 19.1 fusion.75
  2004.1 18.8 fusion.81
  2022.9 30.5 %add_convert_fusion = bf16[4,1024,2048]{2,1,0:T(8,128)(2,1)} fusion(f32[4,1024,2048]{2,1,0:T(8,128)} %fusion.75, f32[4,1024,2048]{2,1,0:T(8,128)} %fusion.81, bf16[4,1024,256]{1,2,0:T(8,128)(2,1)} %bitcast.52, bf16[2048,256]{1,0:T(8,128)(2,1)S(1)} %copy-done.61), kind=kOutput, calls=%fused_computation.74 | convolution fusion | flops 4320133120 | bytes 87031808 | tf_op jit(solution)/shard_map/rso,do->rsd/dot_general | solution.py:309
  2053.5 31.2 %reduce-scatter.13.cloned.1.call-done = bf16[4,256,2048]{2,1,0:T(8,128)(2,1)} async-done(((bf16[4,1024,2048]{2,1,0:T(8,128)(2,1)}), bf16[4,256,2048]{2,1,0:T(8,128)(2,1)}) %reduce-scatter.13.cloned.1.call-update) | async-done | bytes 4194320 | tf_op jit(solution)/shard_map/reduce_scatter | solution.py:215
  2084.7 6.9 multiply_convert_fusion.3
  2091.6 59.7 %all-reduce.11.cloned.1.call-done = (bf16[8,16,512]{2,0,1:T(8,128)(2,1)}, bf16[8,16,256]{2,0,1:T(8,128)(2,1)}, bf16[8,16,256]{2,0,1:T(8,128)(2,1)}, bf16[8,512,1...) async-done(((bf16[8,16,512]{2,0,1:T(8,128)(2,1)}, bf16[8,16,256]{2,0,1:T(8,128)(2,1)}, ...) | async-done | bytes 1572880 | tf_op jit(solution)/shard_map/psum | solution.py:343
  2163.7 163.2 %all-reduce.9.cloned.1.call-done = (f32[8,2048,16]{1,0,2:T(8,128)}, f32[8,2048,16]{1,0,2:T(8,128)}, f32[8,2048,16]{1,0,2:T(8,128)}, f32[8,16,2048]{2,0,1:T(8,128...) async-done(((f32[8,2048,16]{1,0,2:T(8,128)}, f32[8,2048,16]{1,0,2:T(8,128)}, f32[8,2048,16]{1,0,2:T(8,128)}, f32[8,16,2048]{2,0,1:T(8,128)}, ...) | async-done | bytes 7340048 | tf_op jit(solution)/shard_map/psum | solution.py:351
  2343.3 140.4 %reduce-scatter.21.cloned.1.call-done = bf16[4,256,2048]{2,1,0:T(8,128)(2,1)} async-done(((bf16[4,1024,2048]{2,1,0:T(8,128)(2,1)}), bf16[4,256,2048]{2,1,0:T(8,128)(2,1)}) %reduce-scatter.21.cloned.1.call-update) | async-done | bytes 4194320 | tf_op jit(solution)/shard_map/reduce_scatter | solution.py:328
  2483.7 6.8 fusion.54
  2490.6 15.1 fusion.50
  (477 shorter events, 333.5 us)
Async XLA Ops:
  7.2 336.3 %copy-start = (bf16[512,2048]{1,0:T(8,128)(2,1)S(1)}, bf16[512,2048]{1,0:T(8,128)(2,1)}, u32[]{:S(2)}) copy-start(bf16[512,2048]{1,0:T(8,128)(2,1)} %param.56) | copy-start | bytes 6291460
  7.2 169.5 %all-gather.5.cloned.1.call-start = ((), (), s32[]{:S(2)}) async-start(), calls=%async_computation.8 | async-start | bytes 20971520 | tf_op jit(solution)/shard_map/all_gather | solution.py:154
  16.5 351.4 %reduce-scatter.11.cloned.1.call-start = ((), (), s32[]{:S(2)}) async-start(), calls=%async_computation.10 | async-start | bytes 327680 | tf_op jit(solution)/shard_map/reduce_scatter | solution.py:182
  16.6 14.3 copy-start.107
  26.2 183.2 %copy-start.111 = (f32[128]{0:T(128)}, f32[128]{0:T(128)S(1)}, u32[]{:S(2)}) copy-start(f32[128]{0:T(128)S(1)} %convert_element_type.232) | copy-start | bytes 1540
  28.9 210.8 %copy-start.109 = (f32[128]{0:T(128)}, f32[128]{0:T(128)S(1)}, u32[]{:S(2)}) copy-start(f32[128]{0:T(128)S(1)} %convert_element_type.228) | copy-start | bytes 1540
  34.0 205.7 %copy-start.20 = (f32[1024,128]{0,1:T(8,128)}, f32[1024,128]{0,1:T(8,128)S(1)}, u32[]{:S(2)}) copy-start(f32[1024,128]{0,1:T(8,128)S(1)} %get-tuple-element.270) | copy-start | bytes 1572868
  34.0 225.5 %copy-start.71 = (pred[4]{0:T(512)(128)(4,1)}, pred[4]{0:T(512)(128)(4,1)S(1)}, u32[]{:S(2)}) copy-start(pred[4]{0:T(512)(128)(4,1)S(1)} %compare_and_fusion) | copy-start | bytes 16
  36.4 156.0 %copy-start.42 = (bf16[4,2048,16]{1,2,0:T(8,128)(2,1)S(1)}, bf16[4,2048,16]{1,2,0:T(8,128)(2,1)}, u32[]{:S(2)}) copy-start(bf16[4,2048,16]{1,2,0:T(8,128)(2,1)} %get-tuple-element.256) | copy-start | bytes 786436
  36.4 156.0 %copy-start.44 = (bf16[4,2048,16]{1,2,0:T(8,128)(2,1)S(1)}, bf16[4,2048,16]{1,2,0:T(8,128)(2,1)}, u32[]{:S(2)}) copy-start(bf16[4,2048,16]{1,2,0:T(8,128)(2,1)} %get-tuple-element.257) | copy-start | bytes 786436
  176.7 15.8 copy-start.46
  201.4 58.1 %copy-start.38 = (bf16[4,1024,48]{1,2,0:T(8,128)(2,1)}, bf16[4,1024,48]{1,2,0:T(8,128)(2,1)S(1)}, u32[]{:S(2)}) copy-start(bf16[4,1024,48]{1,2,0:T(8,128)(2,1)S(1)} %convolution_convert_fusion.4) | copy-start | bytes 1179652
  246.8 17.0 copy-start.114
  263.8 76.0 %copy-start.34 = (bf16[4,512,16]{1,2,0:T(8,128)(2,1)S(1)}, bf16[4,512,16]{1,2,0:T(8,128)(2,1)}, u32[]{:S(2)}) copy-start(bf16[4,512,16]{1,2,0:T(8,128)(2,1)} %gather_fusion.6) | copy-start | bytes 196612
  263.8 76.0 %copy-start.72 = (pred[4]{0:T(512)(128)(4,1)S(1)}, pred[4]{0:T(512)(128)(4,1)}, u32[]{:S(2)}) copy-start(pred[4]{0:T(512)(128)(4,1)} %copy-done.71) | copy-start | bytes 16
  343.4 316.1 %reduce-scatter.9.cloned.1.call-start = ((), (), s32[]{:S(2)}) async-start(), calls=%async_computation.9 | async-start | bytes 41943040 | tf_op jit(solution)/shard_map/reduce_scatter | solution.py:181
  361.3 470.7 %all-gather.7.cloned.1.call-start = ((), (), s32[]{:S(2)}) async-start(), calls=%async_computation.11 | async-start | bytes 20971520 | tf_op jit(solution)/shard_map/all_gather | solution.py:192
  362.9 304.5 %copy-start.54 = (bf16[4,16,2048]{2,1,0:T(8,128)(2,1)}, bf16[4,16,2048]{2,1,0:T(8,128)(2,1)S(1)}, u32[]{:S(2)}) copy-start(bf16[4,16,2048]{2,1,0:T(8,128)(2,1)S(1)} %gather_fusion.7) | copy-start | bytes 786436
  362.9 304.6 %copy-start.92 = (f32[2048]{0:T(1024)}, f32[2048]{0:T(1024)S(1)}, u32[]{:S(2)}) copy-start(f32[2048]{0:T(1024)S(1)} %convert_element_type.234) | copy-start | bytes 24580
  673.6 317.4 %all-gather.9.cloned.1.call-start = ((), (), s32[]{:S(2)}) async-start(), calls=%async_computation.14 | async-start | bytes 20971520 | tf_op jit(solution)/shard_map/all_gather | solution.py:236
  679.3 454.0 %reduce-scatter.19.cloned.1.call-start = ((), (), s32[]{:S(2)}) async-start(), calls=%async_computation.16 | async-start | bytes 655360 | tf_op jit(solution)/shard_map/reduce_scatter | solution.py:265
  680.0 160.6 %copy-start.24 = (bf16[4,1536,16]{1,2,0:T(8,128)(2,1)}, bf16[4,1536,16]{1,2,0:T(8,128)(2,1)S(1)}, u32[]{:S(2)}) copy-start(bf16[4,1536,16]{1,2,0:T(8,128)(2,1)S(1)} %gather_fusion.11) | copy-start | bytes 589828
  680.5 172.6 %copy-start.26 = (bf16[4,1536,16]{1,2,0:T(8,128)(2,1)}, bf16[4,1536,16]{1,2,0:T(8,128)(2,1)S(1)}, u32[]{:S(2)}) copy-start(bf16[4,1536,16]{1,2,0:T(8,128)(2,1)S(1)} %gather_fusion.10) | copy-start | bytes 589828
  684.1 26.8 %copy-start.22 = (bf16[4,1536,16]{1,2,0:T(8,128)(2,1)}, bf16[4,1536,16]{1,2,0:T(8,128)(2,1)S(1)}, u32[]{:S(2)}) copy-start(bf16[4,1536,16]{1,2,0:T(8,128)(2,1)S(1)} %gather_fusion.12) | copy-start | bytes 589828
  700.2 131.8 %copy-start.48 = (bf16[4,2048,16]{1,2,0:T(8,128)(2,1)S(1)}, bf16[4,2048,16]{1,2,0:T(8,128)(2,1)}, u32[]{:S(2)}) copy-start(bf16[4,2048,16]{1,2,0:T(8,128)(2,1)} %get-tuple-element.255) | copy-start | bytes 786436
  700.2 131.8 %copy-start.50 = (bf16[4,2048,16]{1,2,0:T(8,128)(2,1)S(1)}, bf16[4,2048,16]{1,2,0:T(8,128)(2,1)}, u32[]{:S(2)}) copy-start(bf16[4,2048,16]{1,2,0:T(8,128)(2,1)} %get-tuple-element.258) | copy-start | bytes 786436
  936.5 107.8 %copy-start.27 = (bf16[4,1536,16]{1,2,0:T(8,128)(2,1)S(1)}, bf16[4,1536,16]{1,2,0:T(8,128)(2,1)}, u32[]{:S(2)}) copy-start(bf16[4,1536,16]{1,2,0:T(8,128)(2,1)} %copy-done.26) | copy-start | bytes 589828
  936.5 107.8 %copy-start.73 = (pred[4]{0:T(512)(128)(4,1)S(1)}, pred[4]{0:T(512)(128)(4,1)}, u32[]{:S(2)}) copy-start(pred[4]{0:T(512)(128)(4,1)} %copy-done.71) | copy-start | bytes 16
  1052.3 33.8 %copy-start.25 = (bf16[4,1536,16]{1,2,0:T(8,128)(2,1)S(1)}, bf16[4,1536,16]{1,2,0:T(8,128)(2,1)}, u32[]{:S(2)}) copy-start(bf16[4,1536,16]{1,2,0:T(8,128)(2,1)} %copy-done.24) | copy-start | bytes 589828
  1094.8 327.0 %reduce-scatter.17.cloned.1.call-start = ((), (), s32[]{:S(2)}) async-start(), calls=%async_computation.15 | async-start | bytes 41943040 | tf_op jit(solution)/shard_map/reduce_scatter | solution.py:264
  1133.2 288.7 %copy-start.49 = (bf16[4,2048,16]{1,2,0:T(8,128)(2,1)S(1)}, bf16[4,2048,16]{1,2,0:T(8,128)(2,1)}, u32[]{:S(2)}) copy-start(bf16[4,2048,16]{1,2,0:T(8,128)(2,1)} %get-tuple-element.255) | copy-start | bytes 786436
  1133.2 288.7 %copy-start.51 = (bf16[4,2048,16]{1,2,0:T(8,128)(2,1)S(1)}, bf16[4,2048,16]{1,2,0:T(8,128)(2,1)}, u32[]{:S(2)}) copy-start(bf16[4,2048,16]{1,2,0:T(8,128)(2,1)} %get-tuple-element.258) | copy-start | bytes 786436
  1133.2 288.7 %copy-start.93 = (f32[2048]{0:T(1024)S(1)}, f32[2048]{0:T(1024)}, u32[]{:S(2)}) copy-start(f32[2048]{0:T(1024)} %copy-done.92) | copy-start | bytes 24580
  1133.2 296.3 %copy-start.106 = (f32[4,256]{1,0:T(4,128)S(1)}, f32[4,256]{1,0:T(4,128)}, u32[]{:S(2)}) copy-start(f32[4,256]{1,0:T(4,128)} %copy-done.105) | copy-start | bytes 12292
  1133.2 299.6 %copy-start.90 = (f32[4,256]{1,0:T(4,128)S(1)}, f32[4,256]{1,0:T(4,128)}, u32[]{:S(2)}) copy-start(f32[4,256]{1,0:T(4,128)} %copy-done.89) | copy-start | bytes 12292
  1133.2 299.6 %copy-start.95 = (f32[4,256]{1,0:T(4,128)S(1)}, f32[4,256]{1,0:T(4,128)}, u32[]{:S(2)}) copy-start(f32[4,256]{1,0:T(4,128)} %copy-done.94) | copy-start | bytes 12292
  1133.2 464.3 %all-gather.11.cloned.1.call-start = ((), (), s32[]{:S(2)}) async-start(), calls=%async_computation.17 | async-start | bytes 20971520 | tf_op jit(solution)/shard_map/all_gather | solution.py:285
  1439.1 512.0 %reduce-scatter.15.cloned.1.call-start = ((), (), s32[]{:S(2)}) async-start(), calls=%async_computation.13 | async-start | bytes 163840 | tf_op jit(solution)/shard_map/reduce_scatter | solution.py:218
  1447.8 548.3 %reduce-scatter.23.cloned.1.call-start = ((), (), s32[]{:S(2)}) async-start(), calls=%async_computation.19 | async-start | bytes 491520 | tf_op jit(solution)/shard_map/reduce_scatter | solution.py:331
  1463.5 146.4 %copy-start.59 = (bf16[4,1024,16]{1,2,0:T(8,128)(2,1)}, bf16[4,1024,16]{1,2,0:T(8,128)(2,1)S(1)}, u32[]{:S(2)}) copy-start(bf16[4,1024,16]{1,2,0:T(8,128)(2,1)S(1)} %all_gather.23) | copy-start | bytes 393220
  1463.5 146.4 %copy-start.35 = (bf16[4,512,16]{1,2,0:T(8,128)(2,1)S(1)}, bf16[4,512,16]{1,2,0:T(8,128)(2,1)}, u32[]{:S(2)}) copy-start(bf16[4,512,16]{1,2,0:T(8,128)(2,1)} %gather_fusion.6) | copy-start | bytes 196612
  1858.9 17.3 slice-start
  1862.3 30.5 %copy-start.11 = (bf16[4,1024,2,128]{1,3,2,0:T(8,128)(2,1)}, bf16[4,1024,2,128]{1,3,2,0:T(8,128)(2,1)S(1)}, u32[]{:S(2)}) copy-start(bf16[4,1024,2,128]{1,3,2,0:T(8,128)(2,1)S(1)} %fusion.65) | copy-start | bytes 6291460
  1862.3 13.9 slice-start.1
  1898.3 186.5 %reduce-scatter.13.cloned.1.call-start = ((), (), s32[]{:S(2)}) async-start(), calls=%async_computation.12 | async-start | bytes 20971520 | tf_op jit(solution)/shard_map/reduce_scatter | solution.py:215
  1930.8 220.5 %all-reduce.11.cloned.1.call-start = ((), (), s32[]{:S(2)}) async-start(), calls=%async_computation.21 | async-start | bytes 3145728 | tf_op jit(solution)/shard_map/psum | solution.py:343
  1931.7 16.1 slice-start.2
  1931.7 16.1 slice-start.3
  1995.8 331.1 %all-reduce.9.cloned.1.call-start = ((), (), s32[]{:S(2)}) async-start(), calls=%async_computation.20 | async-start | bytes 14680064 | tf_op jit(solution)/shard_map/psum | solution.py:351
  2004.0 18.9 copy-start.61
  2004.1 479.7 %reduce-scatter.21.cloned.1.call-start = ((), (), s32[]{:S(2)}) async-start(), calls=%async_computation.18 | async-start | bytes 20971520 | tf_op jit(solution)/shard_map/reduce_scatter | solution.py:328
  2053.5 31.3 %copy-start.53 = (bf16[4,16,2048]{2,1,0:T(8,128)(2,1)S(1)}, bf16[4,16,2048]{2,1,0:T(8,128)(2,1)}, u32[]{:S(2)}) copy-start(bf16[4,16,2048]{2,1,0:T(8,128)(2,1)} %copy-done.52) | copy-start | bytes 786436
  2053.5 31.3 %copy-start.85 = (bf16[4,256,16]{1,2,0:T(8,128)(2,1)S(1)}, bf16[4,256,16]{1,2,0:T(8,128)(2,1)}, u32[]{:S(2)}) copy-start(bf16[4,256,16]{1,2,0:T(8,128)(2,1)} %reduce-scatter.15.cloned.1.call-done) | copy-start | bytes 98308
  2053.5 31.3 %copy-start.91 = (f32[4,256]{1,0:T(4,128)S(1)}, f32[4,256]{1,0:T(4,128)}, u32[]{:S(2)}) copy-start(f32[4,256]{1,0:T(4,128)} %copy-done.89) | copy-start | bytes 12292
  2155.3 328.4 %copy-start.43 = (bf16[4,2048,16]{1,2,0:T(8,128)(2,1)S(1)}, bf16[4,2048,16]{1,2,0:T(8,128)(2,1)}, u32[]{:S(2)}) copy-start(bf16[4,2048,16]{1,2,0:T(8,128)(2,1)} %get-tuple-element.256) | copy-start | bytes 786436
  2155.3 328.4 %copy-start.45 = (bf16[4,2048,16]{1,2,0:T(8,128)(2,1)S(1)}, bf16[4,2048,16]{1,2,0:T(8,128)(2,1)}, u32[]{:S(2)}) copy-start(bf16[4,2048,16]{1,2,0:T(8,128)(2,1)} %get-tuple-element.257) | copy-start | bytes 786436
  2155.3 328.4 %copy-start.47 = (bf16[4,2048,16]{1,2,0:T(8,128)(2,1)S(1)}, bf16[4,2048,16]{1,2,0:T(8,128)(2,1)}, u32[]{:S(2)}) copy-start(bf16[4,2048,16]{1,2,0:T(8,128)(2,1)} %get-tuple-element.259) | copy-start | bytes 786436
  2155.3 328.4 %copy-start.67 = (bf16[4,256,48]{1,2,0:T(8,128)(2,1)S(1)}, bf16[4,256,48]{1,2,0:T(8,128)(2,1)}, u32[]{:S(2)}) copy-start(bf16[4,256,48]{1,2,0:T(8,128)(2,1)} %reduce-scatter.23.cloned.1.call-done) | copy-start | bytes 294916
  2155.3 328.4 %copy-start.87 = (f32[2048]{0:T(1024)S(1)}, f32[2048]{0:T(1024)}, u32[]{:S(2)}) copy-start(f32[2048]{0:T(1024)} %copy-done.86) | copy-start | bytes 24580
  2326.9 14.8 copy-start.64
  2343.3 147.3 %copy-start.104 = (f32[4,256]{1,0:T(4,128)S(1)}, f32[4,256]{1,0:T(4,128)}, u32[]{:S(2)}) copy-start(f32[4,256]{1,0:T(4,128)} %copy-done.103) | copy-start | bytes 12292
  2343.3 147.3 %copy-start.96 = (f32[4,256]{1,0:T(4,128)S(1)}, f32[4,256]{1,0:T(4,128)}, u32[]{:S(2)}) copy-start(f32[4,256]{1,0:T(4,128)} %copy-done.94) | copy-start | bytes 12292
  2343.3 147.3 %copy-start.100 = (f32[4,256]{1,0:T(4,128)S(1)}, f32[4,256]{1,0:T(4,128)}, u32[]{:S(2)}) copy-start(f32[4,256]{1,0:T(4,128)} %copy-done.99) | copy-start | bytes 12292
  2343.3 147.3 %copy-start.102 = (f32[4,256]{1,0:T(4,128)S(1)}, f32[4,256]{1,0:T(4,128)}, u32[]{:S(2)}) copy-start(f32[4,256]{1,0:T(4,128)} %copy-done.101) | copy-start | bytes 12292
  (81 other events, 517.9 us)
Sparse Core Ops, SparseCore 0:
  16.6 160.0 all-gather.4
  343.6 24.3 reduce-scatter.10
  371.0 288.5 reduce-scatter.8
  673.7 158.2 all-gather.6
  833.7 157.2 all-gather.8
  1095.0 25.0 reduce-scatter.18
  1133.3 288.4 reduce-scatter.16
  1439.2 158.3 all-gather.10
  1600.8 24.1 reduce-scatter.14
  1898.4 24.6 reduce-scatter.22
  1930.9 153.7 reduce-scatter.12
  2088.6 62.5 all-reduce.10
  2158.9 168.0 all-reduce.8
  2329.8 153.8 reduce-scatter.20
where the time goes:
time: 2520 us; the launch traced here: 2510 us
  waiting for transfers between devices  1430 us (57%)
  matrix products  745 us (30%)
  other arithmetic  175 us (7%)
  local copies, waits for them, and re-layouts  123 us (5%)
    reduce_scatter x1, waiting for transfers between devices, local(): lax.psum_scatter(out_part, 'tensor', scatter_dimension=1, tiled=True)  292 us
    reduce_scatter x1, waiting for transfers between devices, local(): lax.psum_scatter(d_rows, 'tensor', scatter_dimension=1, tiled=True)  289 us
    psum x1, waiting for transfers between devices, local(): lax.psum((grad_a_qkv[..., :rank], grad_a_qkv[..., rank:2 * rank], grad_a_...  163 us
    reduce_scatter x1, waiting for transfers between devices, local(): lax.psum_scatter(d_rows_attn.astype(jnp.bfloat16), 'tensor', scatter_dime...  140 us
    all_gather x1, waiting for transfers between devices, local(): xn_full = lax.all_gather(xn_local, 'tensor', axis=1, tiled=True)  140 us
    all_gather x1, waiting for transfers between devices, local(): lax.all_gather(d_attn, 'tensor', axis=1, tiled=True)  134 us
    all_gather x1, waiting for transfers between devices, local(): ffn_rows = lax.all_gather(x2_local, 'tensor', axis=1, tiled=True)  121 us
    psum x1, waiting for transfers between devices, local(): lax.psum(grad_b_q.astype(jnp.bfloat16), 'dp').astype(jnp.float32)  59.7 us
  transfers between devices with their start and end apart: 14, of which 11 were waited for; matrix products, arithmetic and copies ran while one was open for 28% of the time, Pallas kernels for 0%

commit v1 on v0

v1 whole, which is shorter than its diff:
```python
import functools

import jax
import jax.numpy as jnp
from jax import lax
from jax.experimental import pallas as pl
from jax.experimental.pallas import tpu as pltpu
from jax.sharding import PartitionSpec as P

epsilon = 1e-06
rope_base = 1000000.0
low = jnp.bfloat16
full = jnp.float32
log2e = 1.4426950408889634
ffn_chunks = 3


def dot_nn(a, b):
    return lax.dot_general(a, b, (((1,), (0,)), ((), ())), preferred_element_type=full)


def dot_nt(a, b):
    return lax.dot_general(a, b, (((1,), (1,)), ((), ())), preferred_element_type=full)


def dot_tn(a, b):
    return lax.dot_general(a, b, (((0,), (0,)), ((), ())), preferred_element_type=full)


def norm_back(values, gain, grad):
    scale = lax.rsqrt(jnp.mean(values * values, axis=-1, keepdims=True) + epsilon)
    weighted = grad * gain
    inner = jnp.mean(values * weighted, axis=-1, keepdims=True)
    return scale * weighted - values * (scale * scale * scale * inner)


def normed(values, gain):
    return values * lax.rsqrt(jnp.mean(values * values, axis=-1, keepdims=True) + epsilon) * gain


def rope_tables(slot_count, head_dim):
    position = jnp.arange(slot_count).astype(full)
    exponent = jnp.arange(head_dim // 2).astype(full) * (2.0 / head_dim)
    angles = position[:, None] * (rope_base ** (-exponent))[None, :]
    cosine = jnp.cos(angles)
    sine = jnp.sin(angles)
    return (jnp.concatenate([cosine, cosine], -1), jnp.concatenate([-sine, sine], -1))


def project_kernel(x_ref, h_ref, w_ref, out_ref, *, half, low_half, group, head_dim):
    width = x_ref.shape[1]
    total = dot_nn(x_ref[:, :half], w_ref[0, 0, :half, :])
    total = total + dot_nn(x_ref[:, half:], w_ref[0, 1, :half, :])
    low_rank = 2 * low_half
    table = jnp.concatenate([w_ref[0, 0, half:, :], w_ref[0, 1, half:, :]], axis=0)
    q_width = group * head_dim
    bounds = ((0, q_width), (q_width, q_width + head_dim), (q_width + head_dim, q_width + 2 * head_dim))
    for kind, (start, stop) in enumerate(bounds):
        extra = dot_nn(h_ref[:, kind * low_rank : (kind + 1) * low_rank], table[:, start:stop])
        out_ref[0, :, start:stop] = (total[:, start:stop] + extra).astype(low)


def project(x, h, w_all, group, head_dim):
    tokens, width = x.shape
    tensor_size, _, rows, columns = w_all.shape
    block = (group + 2) * head_dim
    half = width // 2
    return pl.pallas_call(
        functools.partial(
            project_kernel, half=half, low_half=rows - half, group=group, head_dim=head_dim
        ),
        grid=(tensor_size, columns // block),
        in_specs=[
            pl.BlockSpec((tokens, width), lambda t, j: (0, 0)),
            pl.BlockSpec(h.shape, lambda t, j: (0, 0)),
            pl.BlockSpec((1, 2, rows, block), lambda t, j: (t, 0, 0, j)),
        ],
        out_specs=pl.BlockSpec((1, tokens, block), lambda t, j: (t, 0, j)),
        out_shape=jax.ShapeDtypeStruct((tensor_size, tokens, columns), low),
        name="project",
    )(x, h, w_all)


def project_back_kernel(
    d_ref, w_ref, ht_ref, dx_ref, dh_ref, gb_ref, *, half, low_half, group, head_dim
):
    step = pl.program_id(0) * pl.num_programs(1) + pl.program_id(1)

    @pl.when(step == 0)
    def _():
        dx_ref[...] = jnp.zeros_like(dx_ref)
        dh_ref[...] = jnp.zeros_like(dh_ref)

    grad = d_ref[0]
    dx_ref[:, :half] += dot_nt(grad, w_ref[0, 0, :half, :])
    dx_ref[:, half:] += dot_nt(grad, w_ref[0, 1, :half, :])
    low_rank = 2 * low_half
    table = jnp.concatenate([w_ref[0, 0, half:, :], w_ref[0, 1, half:, :]], axis=0)
    q_width = group * head_dim
    bounds = ((0, q_width), (q_width, q_width + head_dim), (q_width + head_dim, q_width + 2 * head_dim))
    for kind, (start, stop) in enumerate(bounds):
        columns = slice(kind * low_rank, (kind + 1) * low_rank)
        dh_ref[:, columns] += dot_nt(grad[:, start:stop], table[:, start:stop])
        gb_ref[0, :, start:stop] = dot_nn(ht_ref[columns, :], grad[:, start:stop]).astype(low)


def project_back(d_qkv, w_all, h_t, group, head_dim):
    tensor_size, tokens, columns = d_qkv.shape
    rows = w_all.shape[2]
    block = (group + 2) * head_dim
    low_all = h_t.shape[0]
    low_rank = low_all // 3
    half = rows - low_rank // 2
    return pl.pallas_call(
        functools.partial(
            project_back_kernel, half=half, low_half=rows - half, group=group, head_dim=head_dim
        ),
        grid=(tensor_size, columns // block),
        in_specs=[
            pl.BlockSpec((1, tokens, block), lambda t, j: (t, 0, j)),
            pl.BlockSpec((1, 2, rows, block), lambda t, j: (t, 0, 0, j)),
            pl.BlockSpec(h_t.shape, lambda t, j: (0, 0)),
        ],
        out_specs=[
            pl.BlockSpec((tokens, 2 * half), lambda t, j: (0, 0)),
            pl.BlockSpec((tokens, low_all), lambda t, j: (0, 0)),
            pl.BlockSpec((1, low_rank, block), lambda t, j: (t, 0, j)),
        ],
        out_shape=[
            jax.ShapeDtypeStruct((tokens, 2 * half), full),
            jax.ShapeDtypeStruct((tokens, low_all), full),
            jax.ShapeDtypeStruct((tensor_size, low_rank, columns), low),
        ],
        name="project_back",
    )(d_qkv, w_all, h_t)


def turned_head(raw, gain, cosine, sine):
    value = normed(raw, gain)
    return value * cosine + pltpu.roll(value, value.shape[-1] // 2, 1) * sine


def turned_head_back(raw, gain, cosine, sine, grad):
    grad = grad * cosine + pltpu.roll(grad * sine, grad.shape[-1] // 2, 1)
    return norm_back(raw, gain, grad)


def attend_kernel(
    len_ref, qkv_ref, qg_ref, kg_ref, cos_ref, sin_ref, out_ref, q_s, k_s, *, group, q_block
):
    shards, _, shard_len, _ = qkv_ref.shape
    slots = shards * shard_len
    head_dim = qg_ref.shape[1]
    scale = head_dim ** (-0.5) * log2e
    cosine = cos_ref[...]
    sine = sin_ref[...]

    def part(index):
        return qkv_ref[:, 0, :, index * head_dim : (index + 1) * head_dim].reshape(slots, head_dim)

    for g in range(group):
        q_s[g] = turned_head(part(g).astype(full), qg_ref[...], cosine, sine).astype(low)
    k_s[...] = turned_head(part(group).astype(full), kg_ref[...], cosine, sine).astype(low)
    value = part(group + 1)
    length = len_ref[pl.program_id(0)]
    per_shard = shard_len // q_block if shard_len >= q_block else 1
    shard_step = 1 if shard_len >= q_block else q_block // shard_len
    for b in range(slots // q_block):
        stop = (b + 1) * q_block
        if shard_len >= q_block:
            rows = (slice(b // per_shard, b // per_shard + 1),)
            inner = slice((b % per_shard) * q_block, (b % per_shard + 1) * q_block)
        else:
            rows = (slice(b * shard_step, (b + 1) * shard_step),)
            inner = slice(0, shard_len)

        def write(columns, block):
            out_ref[rows[0], 0, inner, columns] = block.reshape(
                rows[0].stop - rows[0].start, inner.stop - inner.start, head_dim
            )

        @pl.when(b * q_block < length)
        def _():
            keep = lax.broadcasted_iota(jnp.int32, (q_block, q_block), 1) <= lax.broadcasted_iota(
                jnp.int32, (q_block, q_block), 0
            )
            for g in range(group):
                scores = dot_nt(q_s[g, b * q_block : stop, :], k_s[:stop, :])
                terms = jnp.exp2(scores * scale)
                diagonal = jnp.where(keep, terms[:, b * q_block :], 0.0)
                if b:
                    terms = jnp.concatenate([terms[:, : b * q_block], diagonal], axis=1)
                else:
                    terms = diagonal
                total = jnp.sum(terms, axis=1, keepdims=True)
                mixed = dot_nn(terms.astype(low), value[:stop, :]) / total
                write(slice(g * head_dim, (g + 1) * head_dim), mixed.astype(low))

        @pl.when(b * q_block >= length)
        def _():
            for g in range(group):
                write(
                    slice(g * head_dim, (g + 1) * head_dim), jnp.zeros((q_block, head_dim), low)
                )


def attend(qkv, lengths, q_gain, k_gain, cosine, sine, group):
    shards, rows, shard_len, columns = qkv.shape
    head_dim = q_gain.shape[1]
    block = (group + 2) * head_dim
    heads = columns // block
    slots = shards * shard_len
    q_block = min(256, slots)
    table = pl.BlockSpec((slots, head_dim), lambda r, h, lens: (0, 0))
    gain = pl.BlockSpec((1, head_dim), lambda r, h, lens: (0, 0))
    return pl.pallas_call(
        functools.partial(attend_kernel, group=group, q_block=q_block),
        grid_spec=pltpu.PrefetchScalarGridSpec(
            num_scalar_prefetch=1,
            grid=(rows, heads),
            in_specs=[
                pl.BlockSpec((shards, 1, shard_len, block), lambda r, h, lens: (0, r, 0, h)),
                gain,
                gain,
                table,
                table,
            ],
            out_specs=pl.BlockSpec(
                (shards, 1, shard_len, group * head_dim), lambda r, h, lens: (0, r, 0, h)
            ),
            scratch_shapes=[
                pltpu.VMEM((group, slots, head_dim), low),
                pltpu.VMEM((slots, head_dim), low),
            ],
        ),
        out_shape=jax.ShapeDtypeStruct((shards, rows, shard_len, heads * group * head_dim), low),
        name="attend",
    )(lengths, qkv, q_gain, k_gain, cosine, sine)


def attend_back_kernel(
    len_ref,
    qkv_ref,
    do_ref,
    qg_ref,
    kg_ref,
    cos_ref,
    sin_ref,
    out_ref,
    q_s,
    k_s,
    kt_s,
    dq_s,
    dk_s,
    dv_s,
    *,
    group,
    q_block,
):
    shards, _, shard_len, _ = qkv_ref.shape
    slots = shards * shard_len
    head_dim = qg_ref.shape[1]
    scale = head_dim ** (-0.5)

    def part(ref, index):
        return ref[:, 0, :, index * head_dim : (index + 1) * head_dim].reshape(slots, head_dim)

    def put(index, block):
        out_ref[:, 0, :, index * head_dim : (index + 1) * head_dim] = block.astype(low).reshape(
            shards, shard_len, head_dim
        )

    for g in range(group):
        q_s[g] = turned_head(
            part(qkv_ref, g).astype(full), qg_ref[...], cos_ref[...], sin_ref[...]
        ).astype(low)
    k_rot = turned_head(
        part(qkv_ref, group).astype(full), kg_ref[...], cos_ref[...], sin_ref[...]
    )
    k_s[...] = k_rot.astype(low)
    kt_s[...] = k_rot.T.astype(low)
    dk_s[...] = jnp.zeros_like(dk_s)
    dv_s[...] = jnp.zeros_like(dv_s)
    value = part(qkv_ref, group + 1)
    length = len_ref[pl.program_id(0)]
    for b in range(slots // q_block):
        start = b * q_block
        stop = start + q_block

        @pl.when(start < length)
        def _():
            keep = lax.broadcasted_iota(jnp.int32, (q_block, q_block), 0) <= lax.broadcasted_iota(
                jnp.int32, (q_block, q_block), 1
            )
            for g in range(group):
                q_rows = q_s[g, start:stop, :]
                d_rows = part(do_ref, g)[start:stop, :]
                scores = dot_nt(k_s[:stop, :], q_rows)
                terms = jnp.exp2(scores * (scale * log2e))
                diagonal = jnp.where(keep, terms[start:, :], 0.0)
                if b:
                    terms = jnp.concatenate([terms[:start, :], diagonal], axis=0)
                else:
                    terms = diagonal
                p = terms * (1.0 / jnp.sum(terms, axis=0, keepdims=True))
                dp = dot_nt(value[:stop, :], d_rows)
                inner = jnp.sum(p * dp, axis=0, keepdims=True)
                ds = (p * (dp - inner)).astype(low)
                dq_s[g, start:stop, :] = dot_nn(kt_s[:, :stop], ds).T * scale
                dk_s[:stop, :] += dot_nn(ds, q_rows)
                dv_s[:stop, :] += dot_nn(p.astype(low), d_rows)

        @pl.when(start >= length)
        def _():
            for g in range(group):
                dq_s[g, start:stop, :] = jnp.zeros((q_block, head_dim), full)

    for g in range(group):
        put(
            g,
            turned_head_back(
                part(qkv_ref, g).astype(full), qg_ref[...], cos_ref[...], sin_ref[...], dq_s[g]
            ),
        )
    put(
        group,
        turned_head_back(
            part(qkv_ref, group).astype(full),
            kg_ref[...],
            cos_ref[...],
            sin_ref[...],
            dk_s[...] * scale,
        ),
    )
    put(group + 1, dv_s[...])


def attend_back(qkv, d_attended, lengths, q_gain, k_gain, cosine, sine, group):
    shards, rows, shard_len, columns = qkv.shape
    head_dim = q_gain.shape[1]
    block = (group + 2) * head_dim
    heads = columns // block
    slots = shards * shard_len
    q_block = min(256, slots)
    table = pl.BlockSpec((slots, head_dim), lambda r, h, lens: (0, 0))
    gain = pl.BlockSpec((1, head_dim), lambda r, h, lens: (0, 0))
    wide = pl.BlockSpec((shards, 1, shard_len, block), lambda r, h, lens: (0, r, 0, h))
    return pl.pallas_call(
        functools.partial(attend_back_kernel, group=group, q_block=q_block),
        grid_spec=pltpu.PrefetchScalarGridSpec(
            num_scalar_prefetch=1,
            grid=(rows, heads),
            in_specs=[
                wide,
                pl.BlockSpec(
                    (shards, 1, shard_len, group * head_dim), lambda r, h, lens: (0, r, 0, h)
                ),
                gain,
                gain,
                table,
                table,
            ],
            out_specs=wide,
            scratch_shapes=[
                pltpu.VMEM((group, slots, head_dim), low),
                pltpu.VMEM((slots, head_dim), low),
                pltpu.VMEM((head_dim, slots), low),
                pltpu.VMEM((group, slots, head_dim), full),
                pltpu.VMEM((slots, head_dim), full),
                pltpu.VMEM((slots, head_dim), full),
            ],
        ),
        out_shape=jax.ShapeDtypeStruct(qkv.shape, low),
        name="attend_back",
    )(lengths, qkv, d_attended, q_gain, k_gain, cosine, sine)


def ffn_kernel(
    x_ref,
    dy_ref,
    hg_ref,
    hu_ref,
    dh_ref,
    hgt_ref,
    hut_ref,
    dht_ref,
    w_ref,
    y_ref,
    dx_ref,
    yl_ref,
    dgl_ref,
    dul_ref,
    gb_ref,
    act_s,
    dgate_s,
    dup_s,
    *,
    token_block,
):
    tokens, width = x_ref.shape

    @pl.when(pl.program_id(0) == 0)
    def _():
        y_ref[...] = jnp.zeros_like(y_ref)
        dx_ref[...] = jnp.zeros_like(dx_ref)
        yl_ref[...] = jnp.zeros_like(yl_ref)
        dgl_ref[...] = jnp.zeros_like(dgl_ref)
        dul_ref[...] = jnp.zeros_like(dul_ref)

    def block(i, carry):
        rows = pl.ds(pl.multiple_of(i * token_block, token_block), token_block)
        x = x_ref[rows, :]
        dy = dy_ref[rows, :]
        gate = dot_nt(x, w_ref[0, 0, :, :width]) + dot_nt(hg_ref[rows, :], w_ref[0, 0, :, width:])
        up = dot_nt(x, w_ref[0, 1, :, :width]) + dot_nt(hu_ref[rows, :], w_ref[0, 1, :, width:])
        dact = dot_nt(dy, w_ref[0, 2, :, :width]) + dot_nt(dh_ref[rows, :], w_ref[0, 2, :, width:])
        sig = 1.0 / (1.0 + jnp.exp(-gate))
        silu = gate * sig
        act = (silu * up).astype(low)
        dgate = (dact * up * (sig * (1.0 + gate * (1.0 - sig)))).astype(low)
        dup = (dact * silu).astype(low)
        act_s[rows, :] = act
        dgate_s[rows, :] = dgate
        dup_s[rows, :] = dup
        y_ref[rows, :] += dot_nn(act, w_ref[0, 2, :, :width])
        yl_ref[rows, :] += dot_nn(act, w_ref[0, 2, :, width:])
        dx_ref[rows, :] += dot_nn(dgate, w_ref[0, 0, :, :width]) + dot_nn(
            dup, w_ref[0, 1, :, :width]
        )
        dgl_ref[rows, :] += dot_nn(dgate, w_ref[0, 0, :, width:])
        dul_ref[rows, :] += dot_nn(dup, w_ref[0, 1, :, width:])
        return carry

    lax.fori_loop(0, tokens // token_block, block, 0)
    gb_ref[0, 0] = dot_nn(hgt_ref[...], dgate_s[...]).astype(low)
    gb_ref[0, 1] = dot_nn(hut_ref[...], dup_s[...]).astype(low)
    gb_ref[0, 2] = dot_nn(dht_ref[...], act_s[...]).astype(low)


def ffn(x, dy, h_gate, h_up, dh_down, weights):
    tokens, width = x.shape
    blocks, kinds, units, augmented = weights.shape
    low_all = augmented - width
    token_block = min(512, tokens)

    def whole(array):
        return pl.BlockSpec(array.shape, lambda b: (0, 0), pipeline_mode=pl.Buffered(1))

    def kept(shape):
        return pl.BlockSpec(shape, lambda b: (0, 0), pipeline_mode=pl.Buffered(1))

    wide = (tokens, width)
    thin = (tokens, low_all)
    inputs = (x, dy, h_gate, h_up, dh_down, h_gate.T, h_up.T, dh_down.T)
    return pl.pallas_call(
        functools.partial(ffn_kernel, token_block=token_block),
        grid=(blocks,),
        in_specs=[whole(item) for item in inputs]
        + [pl.BlockSpec((1, kinds, units, augmented), lambda b: (b, 0, 0, 0))],
        out_specs=[
            kept(wide),
            kept(wide),
            kept(thin),
            kept(thin),
            kept(thin),
            pl.BlockSpec((1, kinds, low_all, units), lambda b: (b, 0, 0, 0)),
        ],
        out_shape=[
            jax.ShapeDtypeStruct(wide, full),
            jax.ShapeDtypeStruct(wide, full),
            jax.ShapeDtypeStruct(thin, full),
            jax.ShapeDtypeStruct(thin, full),
            jax.ShapeDtypeStruct(thin, full),
            jax.ShapeDtypeStruct((blocks, kinds, low_all, units), low),
        ],
        scratch_shapes=[pltpu.VMEM((tokens, units), low) for _ in range(3)],
        name="ffn",
    )(*inputs, weights)


def local(
    hidden_in,
    cotangent,
    lengths,
    adapter_ids,
    attn_norm,
    q_norm,
    k_norm,
    ffn_norm,
    w_q,
    key_weight,
    value_weight,
    w_o,
    w_gate,
    w_up,
    w_down,
    a_q,
    b_q,
    a_k,
    key_second_factor,
    a_v,
    value_second_factor,
    a_o,
    b_o,
    a_gate,
    b_gate,
    a_up,
    b_up,
    a_down,
    b_down,
):
    row_count, shard_len, width = hidden_in.shape
    tensor_size = lax.axis_size("tensor")
    dp_size = lax.axis_size("dp")
    head_dim = q_norm.shape[0]
    adapter_count, _, rank = a_q.shape
    low_all = adapter_count * rank
    tokens = row_count * shard_len
    kv_heads = key_weight.shape[1] // head_dim
    group = w_q.shape[1] // key_weight.shape[1]
    units = w_gate.shape[0]
    core = lax.axis_index("dp") % 2
    offset = lax.axis_index("tensor") * shard_len
    pair_groups = [
        [d * tensor_size + t for t in range(tensor_size) for d in (2 * p, 2 * p + 1)]
        for p in range(dp_size // 2)
    ]

    def gather(half):
        return lax.all_gather(
            half, ("dp", "tensor"), axis=0, axis_index_groups=pair_groups
        ).reshape((tensor_size, 2) + half.shape)

    def my_half(array, axis):
        size = array.shape[axis] // 2
        return lax.dynamic_slice_in_dim(array, core * size, size, axis)

    def by_head(q_part, k_part, v_part):
        pieces = []
        for h in range(kv_heads):
            pieces.append(q_part[:, h * group * head_dim : (h + 1) * group * head_dim])
            pieces.append(k_part[:, h * head_dim : (h + 1) * head_dim])
            pieces.append(v_part[:, h * head_dim : (h + 1) * head_dim])
        return jnp.concatenate(pieces, axis=1)

    def flat_a(table):
        return table.transpose(0, 2, 1).reshape(low_all, table.shape[1])

    def flat_b(table):
        return table.reshape(low_all, table.shape[2])

    def flat_mid(table):
        return table.transpose(1, 2, 0).reshape(low_all, table.shape[0])

    def unflat_a(grad):
        return grad.reshape(adapter_count, rank, -1).transpose(0, 2, 1)

    def unflat_b(grad):
        return grad.reshape(adapter_count, rank, -1)

    def unflat_mid(grad):
        return grad.reshape(adapter_count, rank, -1).transpose(2, 0, 1)

    qkv_local = by_head(w_q, key_weight, value_weight)
    qkv_low = by_head(flat_b(b_q), flat_b(key_second_factor), flat_b(value_second_factor))
    qkv_all = gather(jnp.concatenate([my_half(qkv_local, 0), my_half(qkv_low, 0)], axis=0))
    out_local = jnp.concatenate([w_o, flat_a(a_o).T], axis=1)
    out_all = gather(my_half(out_local, 0)).reshape(tensor_size, -1, width + low_all)
    chunk_units = units // ffn_chunks
    ffn_all = []
    tables = (
        (w_gate, flat_mid(b_gate).T),
        (w_up, flat_mid(b_up).T),
        (w_down, flat_mid(a_down).T),
    )
    for c in range(ffn_chunks):
        halves = []
        for main, thin in tables:
            start = c * chunk_units + core * (chunk_units // 2)
            halves.append(
                jnp.concatenate(
                    [
                        lax.dynamic_slice_in_dim(main, start, chunk_units // 2, 0),
                        lax.dynamic_slice_in_dim(thin, start, chunk_units // 2, 0),
                    ],
                    axis=1,
                )
            )
        ffn_all.append(
            gather(jnp.stack(halves)).reshape(
                2 * tensor_size, 3, chunk_units // 2, width + low_all
            )
        )

    cosine, sine = rope_tables(shard_len * tensor_size, head_dim)
    attn_gain = attn_norm.astype(full)
    ffn_gain = ffn_norm.astype(full)
    q_gain = q_norm.astype(full)[None]
    k_gain = k_norm.astype(full)[None]
    slot_local = offset + jnp.arange(shard_len)
    valid = (slot_local[None, :] < lengths[:, None]).astype(full).reshape(tokens, 1)
    mine = jnp.arange(low_all)[None, :] // rank == adapter_ids[:, None]
    mask = jnp.broadcast_to(mine[:, None, :], (row_count, shard_len, low_all)).reshape(
        tokens, low_all
    )

    def masked(values):
        repeated = jnp.concatenate([mask] * (values.shape[1] // low_all), axis=1)
        return jnp.where(repeated, values, 0.0)

    hidden32 = hidden_in.reshape(tokens, width).astype(full)
    d_out = cotangent.reshape(tokens, width).astype(full) * valid
    d_ffn = d_out.astype(low)
    b_down_flat = flat_b(b_down)
    b_o_flat = flat_b(b_o)
    dh_down = masked(dot_nt(d_ffn, b_down_flat)).astype(low)

    xn = normed(hidden32, attn_gain).astype(low)
    a_qkv = jnp.concatenate([flat_a(a_q), flat_a(a_k), flat_a(a_v)], axis=0)
    a_gu = jnp.concatenate([flat_a(a_gate), flat_a(a_up)], axis=0)
    h_qkv = masked(dot_nt(xn, a_qkv)).astype(low)
    sent = project(xn, h_qkv, qkv_all, group, head_dim)
    qkv = lax.all_to_all(sent, "tensor", 0, 0).reshape(
        tensor_size, row_count, shard_len, sent.shape[2]
    )
    attended = attend(qkv, lengths, q_gain, k_gain, cosine, sine, group)
    attn_cat = lax.all_to_all(attended.reshape(tensor_size, tokens, -1), "tensor", 0, 0)
    out_sum = jnp.einsum("tso,tod->sd", attn_cat, out_all, preferred_element_type=full)
    h_o = masked(out_sum[:, width:]).astype(low)
    residual = hidden32 + out_sum[:, :width] + dot_nn(h_o, b_o_flat)
    x2 = normed(residual, ffn_gain).astype(low)
    h_gu = masked(dot_nt(x2, a_gu)).astype(low)
    results = [
        ffn(x2, d_ffn, h_gu[:, :low_all], h_gu[:, low_all:], dh_down, item) for item in ffn_all
    ]
    ffn_sum, d_x2, h_down, dh_gate, dh_up = (
        functools.reduce(lambda a, b: a + b, [item[i] for item in results]) for i in range(5)
    )
    h_down = masked(h_down).astype(low)
    output = ((residual + ffn_sum + dot_nn(h_down, b_down_flat)) * valid).astype(low)
    dh_gu = masked(jnp.concatenate([dh_gate, dh_up], axis=1)).astype(low)
    d_x2 = d_x2 + dot_nn(dh_gu, a_gu)
    d_residual = d_out + norm_back(residual, ffn_gain, d_x2)
    d_attn = d_residual.astype(low)
    dh_o = masked(dot_nt(d_attn, b_o_flat)).astype(low)
    d_cat = jnp.einsum(
        "sd,tod->tso",
        jnp.concatenate([d_attn, dh_o], axis=1),
        out_all,
        preferred_element_type=full,
    ).astype(low)
    d_attended = lax.all_to_all(d_cat, "tensor", 0, 0).reshape(attended.shape)
    d_sent = attend_back(qkv, d_attended, lengths, q_gain, k_gain, cosine, sine, group)
    d_qkv = lax.all_to_all(d_sent.reshape(sent.shape), "tensor", 0, 0)
    d_xn, dh_qkv, grad_b_qkv = project_back(d_qkv, qkv_all, h_qkv.T, group, head_dim)
    dh_qkv = masked(dh_qkv).astype(low)
    d_xn = d_xn + dot_nn(dh_qkv, a_qkv)
    d_input = (d_residual + norm_back(hidden32, attn_gain, d_xn)).astype(low)

    grad_b_down = dot_tn(h_down, d_ffn).astype(low)
    grad_a_gu = dot_tn(dh_gu, x2).astype(low)
    grad_b_o = dot_tn(h_o, d_attn).astype(low)
    grad_a_o = jnp.einsum("sk,tso->tko", dh_o, attn_cat, preferred_element_type=full).astype(low)
    grad_ffn = jnp.stack([item[5] for item in results])
    grad_ffn = grad_ffn.reshape(ffn_chunks, tensor_size, 2, 3, low_all, chunk_units // 2)
    grad_ffn = grad_ffn.transpose(1, 3, 4, 0, 2, 5).reshape(tensor_size, 3 * low_all, units)
    grad_a_qkv = dot_tn(dh_qkv, xn).astype(low)

    def reduce_all(split, whole):
        lengths_split = [item.shape[1] * item.shape[2] for item in split]
        parts = [item.reshape(tensor_size, -1, 128) for item in split]
        joined = jnp.concatenate(whole, axis=0)
        parts.append(joined.reshape(tensor_size, -1, 128))
        sums = lax.psum_scatter(jnp.concatenate(parts, axis=1), "tensor", scatter_dimension=0)
        sums = lax.psum(sums, "dp")
        outs = []
        start = 0
        for item, count in zip(split, lengths_split):
            outs.append(sums[start : start + count // 128].reshape(item.shape[1:]).astype(full))
            start += count // 128
        total = lax.all_gather(sums[start:], "tensor", axis=0).reshape(joined.shape).astype(full)
        return outs, total

    (grad_ffn, grad_a_o), early = reduce_all(
        (grad_ffn, grad_a_o), (grad_b_down, grad_a_gu, grad_b_o)
    )
    (grad_b_qkv,), late = reduce_all((grad_b_qkv,), (grad_a_qkv,))

    def of_kind(array, start, size):
        step = (group + 2) * head_dim
        return jnp.concatenate(
            [array[:, h * step + start : h * step + start + size] for h in range(kv_heads)], axis=1
        )

    def piece(array, index):
        return array[index * low_all : (index + 1) * low_all]

    return (
        output.reshape(hidden_in.shape),
        d_input.reshape(hidden_in.shape),
        unflat_a(piece(late, 0)),
        unflat_b(of_kind(grad_b_qkv, 0, group * head_dim)),
        unflat_a(piece(late, 1)),
        unflat_b(of_kind(grad_b_qkv, group * head_dim, head_dim)),
        unflat_a(piece(late, 2)),
        unflat_b(of_kind(grad_b_qkv, (group + 1) * head_dim, head_dim)),
        unflat_a(grad_a_o),
        unflat_b(piece(early, 3)),
        unflat_a(piece(early, 1)),
        unflat_mid(piece(grad_ffn, 0)),
        unflat_a(piece(early, 2)),
        unflat_mid(piece(grad_ffn, 1)),
        unflat_mid(piece(grad_ffn, 2)),
        unflat_b(piece(early, 0)),
    )


def solution(mesh):
    placed = (
        P("dp", "tensor", None),
        P("dp", "tensor", None),
        P("dp"),
        P("dp"),
        P(),
        P(),
        P(),
        P(),
        P(None, "tensor"),
        P(None, "tensor"),
        P(None, "tensor"),
        P("tensor", None),
        P("tensor", None),
        P("tensor", None),
        P("tensor", None),
        P(),
        P(None, None, "tensor"),
        P(),
        P(None, None, "tensor"),
        P(),
        P(None, None, "tensor"),
        P(None, "tensor", None),
        P(),
        P(),
        P("tensor", None, None),
        P(),
        P("tensor", None, None),
        P("tensor", None, None),
        P(),
    )
    return jax.shard_map(
        local,
        mesh=mesh,
        in_specs=placed,
        out_specs=(
            P("dp", "tensor", None),
            P("dp", "tensor", None),
            P(),
            P(None, None, "tensor"),
            P(),
            P(None, None, "tensor"),
            P(),
            P(None, None, "tensor"),
            P(None, "tensor", None),
            P(),
            P(),
            P("tensor", None, None),
            P(),
            P("tensor", None, None),
            P("tensor", None, None),
            P(),
        ),
        check_vma=False,
    )
```

time: 2520 us -> 1360 us (0.54)
  waiting for transfers between devices: 1430 us -> 533 us
  matrix products: 745 us -> 98.5 us
  Pallas kernels: 0 us -> 365 us
  blocking collectives: 22.8 us -> 158 us
  other arithmetic: 175 us -> 67.5 us
    reduce_scatter x8 -> x0, waiting for transfers between devices: 757 us -> none  [the longest x1 292 us: local(): lax.psum_scatter(out_part, 'tensor', scatter_dimension=1, tiled=True)]
    dot_general x86 -> x15, matrix products: 745 us -> 98.5 us  [the longest x4 44.9 us: dot_nn(): lax.dot_general(a, b, (((1,), (0,)), ((), ())), preferred_element_type=full)]
    pallas_call x0 -> x7, Pallas kernels: none -> 365 us  [the longest x3 235 us: ffn(): pl.pallas_call(functools.partial(ffn_kernel, token_block=token_block), gr...]
    all_gather x4 -> x7, waiting for transfers between devices: 450 us -> 226 us  [the longest x5 187 us: gather(): lax.all_gather(half, ('dp', 'tensor'), axis=0, axis_index_groups=pair_gro...]
    all_to_all x0 -> x2, waiting for transfers between devices: none -> 183 us  [the longest x1 118 us: local(): lax.all_to_all(sent, 'tensor', 0, 0)]
    psum x2 -> x1, waiting for transfers between devices: 223 us -> 56 us  [reduce_all(): sums = lax.psum(sums, 'dp')]
    all_to_all x0 -> x2, blocking collectives: none -> 158 us  [the longest x1 79.3 us: local(): d_attended = lax.all_to_all(d_cat, 'tensor', 0, 0).reshape(attended.shape)]
    convert_element_type x19 -> x13, other arithmetic: 105 us -> 24 us  [the longest x2 9.12 us: local(): d_ffn = d_out.astype(low)]
  transfers between devices with their start and end apart: 14 -> 12, of which waited for: 11 -> 10; matrix products, arithmetic and copies ran while one was open for 28% -> 11% of each run, Pallas kernels for 0% -> 21%
where the time goes in v1:
time: 1360 us
  waiting for transfers between devices  533 us (39%)
  Pallas kernels  365 us (27%)
  blocking collectives  158 us (12%)
  local copies, waits for them, and re-layouts  107 us (8%)
  matrix products  98.5 us (7%)
  other arithmetic  67.5 us (5%)
  between operations  15.8 us (1%)
    pallas_call x3, Pallas kernels, ffn(): pl.pallas_call(functools.partial(ffn_kernel, token_block=token_block), gr...  235 us
    all_gather x5, waiting for transfers between devices, gather(): lax.all_gather(half, ('dp', 'tensor'), axis=0, axis_index_groups=pair_gro...  187 us
    all_to_all x1, waiting for transfers between devices, local(): lax.all_to_all(sent, 'tensor', 0, 0)  118 us
    all_to_all x1, blocking collectives, local(): d_attended = lax.all_to_all(d_cat, 'tensor', 0, 0).reshape(attended.shape)  79.3 us
    all_to_all x1, blocking collectives, local(): d_qkv = lax.all_to_all(d_sent.reshape(sent.shape), 'tensor', 0, 0)  79.1 us
    unnamed x12, waiting for transfers between devices  67.5 us
    all_to_all x1, waiting for transfers between devices, local(): lax.all_to_all(attended.reshape(tensor_size, tokens, -1), 'tensor', 0, 0)  65.3 us
    psum x1, waiting for transfers between devices, reduce_all(): sums = lax.psum(sums, 'dp')  56 us
  transfers between devices with their start and end apart: 12, of which 10 were waited for; matrix products, arithmetic and copies ran while one was open for 11% of the time, Pallas kernels for 21%

profile of v1, /device:TPU:0, one launch (start us, length us, event | category | flops | bytes accessed | tf_op | source)
XLA Modules:
  0.0 1356.4 jit_solution(11485852879318807599)
XLA Ops:
  12.2 2.4 slice_dynamic-update-slice_fusion.1
  14.6 1.9 slice_dynamic-update-slice_fusion.5
  16.5 1.9 slice_dynamic-update-slice_fusion.4
  28.9 3.5 constant_dynamic-slice_fusion.5
  32.4 5.9 constant_dynamic-slice_fusion.3
  38.6 2.1 pad_maximum_fusion.2
  44.0 2.2 pad_maximum_fusion.1
  47.9 2.1 pad_maximum_fusion.3
  50.5 3.3 fusion.1
  55.2 2.0 copy-done.7
  60.2 61.3 %all-gather.15.cloned.1.call-done = bf16[8704,1024]{1,0:T(8,128)(2,1)} async-done(((bf16[1088,1024]{1,0:T(8,128)(2,1)}), bf16[8704,1024]{1,0:T(8,128)(2,1)}) %all-gather.15.cloned.1.call-update) | async-done | bytes 17825808 | tf_op jit(solution)/shard_map/all_gather | solution.py:530
  121.5 25.0 %project.1 = bf16[4,1024,1024]{2,1,0:T(8,128)(2,1)} custom-call(bf16[1024,2048]{1,0:T(8,128)(2,1)} %copy-done.7, bf16[1024,384]{1,0:T(8,128)(2,1)} %copy.162.h_ref, bf16[4,2,1088,1024]{3,2,1,0:T(8,128)(2,1)} %bitcast.183), custom_call_target="tpu_custom_call" | custom-call | tf_op jit(solution)/shard_map/project/pallas_call | solution.py:68
  146.5 5.8 all-to-all-start
  152.4 1.9 fusion.19
  156.2 117.6 %all-to-all-done = bf16[4,1024,1024]{2,1,0:T(8,128)(2,1)} async-done(((bf16[4,1024,1024]{2,1,0:T(8,128)(2,1)}), bf16[4,1024,1024]{2,1,0:T(8,128)(2,1)}, u32[]{:S(2)}, u32[]{:S(2)}) %all-to-all-start) | async-done | bytes 8388640 | tf_op jit(solution)/shard_map/all_to_all | solution.py:623
  273.9 23.2 %attend.1 = bf16[4,4,256,512]{3,2,1,0:T(8,128)(2,1)} custom-call(s32[4]{0:T(128)} %len_ref.3, bf16[4,4,256,1024]{3,2,1,0:T(8,128)(2,1)} %bitcast.11.qkv_ref, f32[1,128]{1,0:T(1,128)} %get-tuple-element.118.qg_ref, f32[1,128]{1,0:T(1,128)} %get-tuple-element.117.kg_ref, f32[1024,128]{1,0:T(8,128)} %get-tuple-element.115.cos_ref, ...), custom_call_target="tpu_custom_call" | custom-call | tf_op jit(solution)/shard_map/attend/pallas_call | solution.py:216
  297.0 5.1 all-to-all-start.1
  302.3 3.0 multiply_convert_fusion.1
  307.6 6.1 fusion.8.dy_ref
  313.8 65.3 %all-to-all-done.1 = bf16[4,1024,512]{2,1,0:T(8,128)(2,1)} async-done(((bf16[4,1024,512]{2,1,0:T(8,128)(2,1)}), bf16[4,1024,512]{2,1,0:T(8,128)(2,1)}, u32[]{:S(2)}, u32[]{:S(2)}) %all-to-all-start.1) | async-done | bytes 4194336 | tf_op jit(solution)/shard_map/all_to_all | solution.py:627
  379.1 15.6 %convolution_bitcast_fusion = f32[1024,2176]{1,0:T(8,128)S(1)} fusion(bf16[4,1024,512]{2,1,0:T(8,128)(2,1)} %all-to-all-done.1, bf16[4,512,2176]{2,1,0:T(8,128)(2,1)} %bitcast.255), kind=kOutput, calls=%fused_computation.24 | convolution fusion | flops 9126805504 | bytes 22020096 | tf_op jit(solution)/shard_map/tso,tod->sd/dot_general | solution.py:628
  394.7 3.3 copy-done.8
  398.2 5.7 multiply_reduce_fusion.1
  404.7 2.7 copy-done.2
  412.0 13.6 all-gather.21.cloned.1.call-done
  425.6 78.1 %ffn.4 = (f32[1024,2048]{1,0:T(8,128)}, f32[1024,2048]{1,0:T(8,128)}, f32[1024,128]{1,0:T(8,128)}, f32[1024,128]{1,0:T(8,128)}, f32[1024,128]{1,0:T(8,128)}, /*index=5*/bf16[8,3,128,256]{3,2,1,0:T(8,128)(2,1)}) custom-call(bf16[1024,2048]{1,0:T(8,128)(2,1)} %copy-done.5, bf16[1024,2048]{1,0:T(8,128)(2,1)} %fusion.8.dy_ref, bf16[1024,128]{1,0:T(8,128)(2,1)} %copy.170.hg_ref, ...), custom_call_target="tpu_custom_call" | custom-call | tf_op jit(solution)/shard_map/ffn/pallas_call | solution.py:455
  503.7 56.3 %all-gather.19.cloned.1.call-done = bf16[24,256,2176]{2,1,0:T(8,128)(2,1)} async-done(((bf16[3,256,2176]{2,1,0:T(8,128)(2,1)}), bf16[24,256,2176]{2,1,0:T(8,128)(2,1)}) %all-gather.19.cloned.1.call-update) | async-done | bytes 26738704 | tf_op jit(solution)/shard_map/all_gather | solution.py:530
  560.0 78.3 %ffn.3 = (f32[1024,2048]{1,0:T(8,128)}, f32[1024,2048]{1,0:T(8,128)}, f32[1024,128]{1,0:T(8,128)}, f32[1024,128]{1,0:T(8,128)}, f32[1024,128]{1,0:T(8,128)}, /*index=5*/bf16[8,3,128,256]{3,2,1,0:T(8,128)(2,1)}) custom-call(bf16[1024,2048]{1,0:T(8,128)(2,1)} %copy-done.5, bf16[1024,2048]{1,0:T(8,128)(2,1)} %fusion.8.dy_ref, bf16[1024,128]{1,0:T(8,128)(2,1)} %copy.170.hg_ref, ...), custom_call_target="tpu_custom_call" | custom-call | tf_op jit(solution)/shard_map/ffn/pallas_call | solution.py:455
  638.3 55.4 %all-gather.23.cloned.1.call-done = bf16[24,256,2176]{2,1,0:T(8,128)(2,1)} async-done(((bf16[3,256,2176]{2,1,0:T(8,128)(2,1)}), bf16[24,256,2176]{2,1,0:T(8,128)(2,1)}) %all-gather.23.cloned.1.call-update) | async-done | bytes 26738704 | tf_op jit(solution)/shard_map/all_gather | solution.py:530
  693.7 78.2 %ffn.5 = (f32[1024,2048]{1,0:T(8,128)}, f32[1024,2048]{1,0:T(8,128)}, f32[1024,128]{1,0:T(8,128)}, f32[1024,128]{1,0:T(8,128)}, f32[1024,128]{1,0:T(8,128)}, /*index=5*/bf16[8,3,128,256]{3,2,1,0:T(8,128)(2,1)}) custom-call(bf16[1024,2048]{1,0:T(8,128)(2,1)} %copy-done.5, bf16[1024,2048]{1,0:T(8,128)(2,1)} %fusion.8.dy_ref, bf16[1024,128]{1,0:T(8,128)(2,1)} %copy.170.hg_ref, ...), custom_call_target="tpu_custom_call" | custom-call | tf_op jit(solution)/shard_map/ffn/pallas_call | solution.py:455
  774.8 2.0 copy.191
  776.8 2.0 copy.193
  780.4 4.6 convolution_convert_fusion.1
  785.1 17.0 %multiply_reduce_fusion = (f32[1024]{0:T(1024)S(1)}, f32[1024,2048]{1,0:T(8,128)}) fusion(f32[1024,2048]{1,0:T(8,128)} %copy-done.2, f32[2048]{0:T(1024)S(1)} %convert_element_type.169, bf16[128,2048]{1,0:T(8,128)(2,1)} %bitcast.221, bf16[128,2048]{1,0:T(8,128)(2,1)} %bitcast.223, pred[1024,256]{0,1:T(8,128)(4,1)S(1)} %copy-done.26, ...), kind=kOutput, calls=%fused_computation.16 | convolution fusion | flops 1089731584 | bytes 43790336 | tf_op jit(solution)/shard_map/dot_general | solution.py:19
  802.1 8.4 fusion.34
  818.6 7.7 maximum_bitcast_fusion
  826.2 8.6 reshape_reshape.7
  834.8 3.6 fusion.13
  840.8 2.9 convolution_convert_fusion.3
  843.7 2.9 pad_maximum_fusion.6
  846.6 2.9 reshape.375
  849.5 5.9 pad_maximum_fusion
  855.6 13.9 %convert_bitcast_fusion = bf16[4,1024,512]{1,2,0:T(8,128)(2,1)S(1)} fusion(bf16[4,512,2176]{2,1,0:T(8,128)(2,1)} %bitcast.256, bf16[1024,128]{1,0:T(8,128)(2,1)S(1)} %copy.194, bf16[1024,2048]{1,0:T(8,128)(2,1)} %copy-done.6), kind=kOutput, calls=%fused_computation.30 | convolution fusion | flops 9137815552 | bytes 17563648 | tf_op jit(solution)/shard_map/sd,tod->tso/dot_general | solution.py:646
  869.5 79.3 %all_to_all.20 = bf16[4,1024,512]{1,2,0:T(8,128)(2,1)} all-to-all(bf16[4,1024,512]{1,2,0:T(8,128)(2,1)S(1)} %convert_bitcast_fusion), channel_id=1, replica_groups=mesh['dp'=8,'tensor'=4] {'tensor'}, dimensions={0} | all-to-all | bytes 8388608 | tf_op jit(solution)/shard_map/all_to_all | solution.py:652
  948.8 6.2 copy.195
  955.1 53.0 %attend_back.1 = bf16[4,4,256,1024]{3,2,1,0:T(8,128)(2,1)} custom-call(s32[4]{0:T(128)} %len_ref.3, bf16[4,4,256,1024]{3,2,1,0:T(8,128)(2,1)} %bitcast.11.qkv_ref, bf16[4,4,256,512]{3,2,1,0:T(8,128)(2,1)} %bitcast.191, f32[1,128]{1,0:T(1,128)} %get-tuple-element.118.qg_ref, f32[1,128]{1,0:T(1,128)} %get-tuple-element.117.kg_ref, ...), custom_call_target="tpu_custom_call" | custom-call | tf_op jit(solution)/shard_map/attend_back/pallas_call | solution.py:348
  1008.1 79.1 %all_to_all.21.d_ref = bf16[4,1024,1024]{2,1,0:T(8,128)(2,1)} all-to-all(bf16[4,1024,1024]{2,1,0:T(8,128)(2,1)} %bitcast.187), channel_id=1, replica_groups=mesh['dp'=8,'tensor'=4] {'tensor'}, dimensions={0} | all-to-all | bytes 16777216 | tf_op jit(solution)/shard_map/all_to_all | solution.py:654
  1087.2 29.4 %project_back.1 = (f32[1024,2048]{1,0:T(8,128)}, f32[1024,384]{1,0:T(8,128)}, bf16[4,128,1024]{2,1,0:T(8,128)(2,1)}) custom-call(bf16[4,1024,1024]{2,1,0:T(8,128)(2,1)} %all_to_all.21.d_ref, bf16[4,2,1088,1024]{3,2,1,0:T(8,128)(2,1)} %bitcast.184, bf16[384,1024]{1,0:T(8,128)(2,1)} %bitcast.207), custom_call_target="tpu_custom_call" | custom-call | tf_op jit(solution)/shard_map/project_back/pallas_call | solution.py:114
  1118.3 5.1 convolution_convert_fusion
  1123.4 2.6 reshape.367
  1126.0 2.3 reshape.366
  1128.3 2.9 pad_maximum_fusion.4
  1131.3 67.4 %reduce-scatter.7.cloned.1.call-done = bf16[1,2560,128]{2,1,0:T(8,128)(2,1)} async-done(((bf16[4,2560,128]{2,1,0:T(8,128)(2,1)}), bf16[1,2560,128]{2,1,0:T(8,128)(2,1)}) %reduce-scatter.7.cloned.1.call-update) | async-done | bytes 655376
  1198.8 14.1 %multiply_convert_fusion = bf16[1024,2048]{1,0:T(8,128)(2,1)} fusion(f32[1024,2048]{1,0:T(8,128)} %copy-done.2, f32[1024,2048]{1,0:T(8,128)} %get-tuple-element.39, f32[1024,2048]{1,0:T(8,128)} %get-tuple-element.37, f32[1024,2048]{1,0:T(8,128)} %get-tuple-element.38, bf16[1024,128]{0,1:T(8,128)(2,1)S(1)} %select_convert_fusion.2, ...), kind=kOutput, calls=%fused_computation.18 | convolution fusion | flops 549453824 | bytes 38539264 | tf_op jit(solution)/shard_map/dot_general | solution.py:19
  1212.9 56.0 %all-reduce.5.cloned.1.call-done = (bf16[2560,128]{1,0:T(8,128)(2,1)}, bf16[7168,128]{1,0:T(8,128)(2,1)}) async-done(((bf16[2560,128]{1,0:T(8,128)(2,1)}, bf16[7168,128]{1,0:T(8,128)(2,1)}), (bf16[2560,128]{1,0:T(8,128)(2,1)}, bf16[7168,128]{1,0:T(8,128)(2,1)})) %all-reduce.5.cloned.1.call-update) | async-done | bytes 2490384 | tf_op jit(solution)/shard_map/psum | solution.py:675
  1270.8 8.1 fusion.4
  1279.7 3.3 fusion.7
  1292.0 9.5 all-gather.25.cloned.1.call-done
  1301.5 2.5 fusion.37
  1304.0 2.4 reshape.368
  1308.6 30.3 %all-gather.27.cloned.1.call-done = bf16[8192,128]{1,0:T(8,128)(2,1)} async-done(((bf16[2048,128]{1,0:T(8,128)(2,1)}), bf16[8192,128]{1,0:T(8,128)(2,1)}) %all-gather.27.cloned.1.call-update) | async-done | bytes 2097168 | tf_op jit(solution)/shard_map/all_gather | solution.py:681
  1339.0 3.1 fusion.36
  1342.1 2.4 reshape.377
  1344.5 2.4 reshape.379
  (237 shorter events, 68.1 us)
Async XLA Ops:
  7.2 391.0 %copy-start = (bf16[8,16,2048]{2,1,0:T(8,128)(2,1)S(1)}, bf16[8,16,2048]{2,1,0:T(8,128)(2,1)}, u32[]{:S(2)}) copy-start(bf16[8,16,2048]{2,1,0:T(8,128)(2,1)} %param.51) | copy-start | bytes 1572868
  7.2 11.2 copy-start.13
  7.2 114.3 %all-gather.15.cloned.1.call-start = ((), (), s32[]{:S(2)}) async-start(), calls=%async_computation.6 | async-start | bytes 20054016 | tf_op jit(solution)/shard_map/all_gather | solution.py:530
  12.2 7.2 copy-start.23
  12.2 8.0 copy-start.24
  22.9 1.7 copy-start.42
  22.9 2.5 copy-start.14
  24.5 289.3 %all-gather.17.cloned.1.call-start = ((), (), s32[]{:S(2)}) async-start(), calls=%async_computation.7 | async-start | bytes 10027008 | tf_op jit(solution)/shard_map/all_gather | solution.py:530
  26.5 399.1 %all-gather.21.cloned.1.call-start = ((), (), s32[]{:S(2)}) async-start(), calls=%async_computation.9 | async-start | bytes 30081024 | tf_op jit(solution)/shard_map/all_gather | solution.py:530
  40.7 519.3 %all-gather.19.cloned.1.call-start = ((), (), s32[]{:S(2)}) async-start(), calls=%async_computation.8 | async-start | bytes 30081024 | tf_op jit(solution)/shard_map/all_gather | solution.py:530
  41.1 2.7 copy-start.11
  46.2 647.5 %all-gather.23.cloned.1.call-start = ((), (), s32[]{:S(2)}) async-start(), calls=%async_computation.10 | async-start | bytes 30081024 | tf_op jit(solution)/shard_map/all_gather | solution.py:530
  47.9 2.2 copy-start.48
  50.1 3.7 copy-start.46
  50.1 4.0 copy-start.3
  53.8 1.3 copy-start.43
  54.0 353.4 %copy-start.25 = (pred[1024,256]{0,1:T(8,128)(4,1)}, pred[1024,256]{0,1:T(8,128)(4,1)S(1)}, u32[]{:S(2)}) copy-start(pred[1024,256]{0,1:T(8,128)(4,1)S(1)} %get-tuple-element.100) | copy-start | bytes 786436
  54.1 3.1 copy-start.31
  54.1 3.1 copy-start.33
  54.1 3.1 copy-start.35
  55.2 2.0 copy-start.7
  59.0 87.5 %copy-start.12 = (bf16[1024,384]{0,1:T(8,128)(2,1)}, bf16[1024,384]{0,1:T(8,128)(2,1)S(1)}, u32[]{:S(2)}) copy-start(bf16[1024,384]{0,1:T(8,128)(2,1)S(1)} %select_convert_fusion.1) | copy-start | bytes 2359300
  146.5 127.3 %all-to-all-start = ((bf16[4,1024,1024]{2,1,0:T(8,128)(2,1)}), bf16[4,1024,1024]{2,1,0:T(8,128)(2,1)}, u32[]{:S(2)}, u32[]{:S(2)}) async-start(bf16[4,1024,1024]{2,1,0:T(8,128)(2,1)} %project.1), calls=%async_computation | async-start | bytes 16777216 | tf_op jit(solution)/shard_map/all_to_all | solution.py:623
  152.4 3.3 copy-start.49
  152.4 3.3 copy-start.50
  297.0 5.1 copy-start.47
  297.0 5.2 copy-start.45
  297.0 82.1 %all-to-all-start.1 = ((bf16[4,1024,512]{2,1,0:T(8,128)(2,1)}), bf16[4,1024,512]{2,1,0:T(8,128)(2,1)}, u32[]{:S(2)}, u32[]{:S(2)}) async-start(bf16[4,1024,512]{2,1,0:T(8,128)(2,1)} %bitcast.192), calls=%async_computation.1 | async-start | bytes 8388608 | tf_op jit(solution)/shard_map/all_to_all | solution.py:627
  302.1 829.2 %reduce-scatter.9.cloned.1.call-start = ((), (), s32[]{:S(2)}) async-start(), calls=%async_computation.14 | async-start | bytes 9175040
  302.3 3.0 copy-start.29
  306.8 7.0 copy-start.9
  394.7 3.4 copy-start.8
  403.9 3.5 copy-start.2
  403.9 3.5 copy-start.27
  403.9 3.5 copy-start.28
  407.4 2.0 copy-start.5
  693.7 78.2 %copy-start.38 = (f32[1024,128]{1,0:T(8,128)S(1)}, f32[1024,128]{1,0:T(8,128)}, u32[]{:S(2)}) copy-start(f32[1024,128]{1,0:T(8,128)} %get-tuple-element.47) | copy-start | bytes 1572868
  693.7 78.4 %copy-start.39 = (f32[1024,128]{1,0:T(8,128)S(1)}, f32[1024,128]{1,0:T(8,128)}, u32[]{:S(2)}) copy-start(f32[1024,128]{1,0:T(8,128)} %get-tuple-element.46) | copy-start | bytes 1572868
  779.0 6.1 copy-start.21
  780.4 4.6 copy-start.22
  780.4 4.6 copy-start.26
  785.0 17.0 %slice-start = ((s8[8388608]{0:T(1024)(128)(4,1)}), s8[4194304]{0:T(1024)(128)(4,1)S(1)}, s32[]{:S(2)}) async-start(s8[8388608]{0:T(1024)(128)(4,1)} %bitcast.181), calls=%async_computation.16 | async-start | bytes 8388608
  785.0 17.0 %slice-start.1 = ((s8[8388608]{0:T(1024)(128)(4,1)}), s8[4194304]{0:T(1024)(128)(4,1)S(1)}, s32[]{:S(2)}) async-start(s8[8388608]{0:T(1024)(128)(4,1)} %bitcast.181), calls=%async_computation.17 | async-start | bytes 8388608
  810.5 3.2 copy-start.6
  812.1 1.6 copy-start.16
  812.1 3.2 copy-start.17
  813.7 3.3 copy-start.18
  834.8 4.1 copy-start.36
  834.8 4.3 copy-start.37
  855.4 343.2 %reduce-scatter.7.cloned.1.call-start = ((), (), s32[]{:S(2)}) async-start(), calls=%async_computation.13 | async-start | bytes 3276800
  1087.2 31.1 %copy-start.20 = (pred[1024,384]{0,1:T(8,128)(4,1)S(1)}, pred[1024,384]{0,1:T(8,128)(4,1)}, u32[]{:S(2)}) copy-start(pred[1024,384]{0,1:T(8,128)(4,1)} %copy-done.19) | copy-start | bytes 1179652
  1131.2 67.5 %copy-start.30 = (bf16[8,16,2048]{2,1,0:T(8,128)(2,1)S(1)}, bf16[8,16,2048]{2,1,0:T(8,128)(2,1)}, u32[]{:S(2)}) copy-start(bf16[8,16,2048]{2,1,0:T(8,128)(2,1)} %param.57) | copy-start | bytes 1572868
  1131.2 137.7 %all-reduce.5.cloned.1.call-start = ((), (), s32[]{:S(2)}) async-start(), calls=%async_computation.15 | async-start | bytes 4980736 | tf_op jit(solution)/shard_map/psum | solution.py:675
  1198.7 102.8 %all-gather.25.cloned.1.call-start = ((), (), s32[]{:S(2)}) async-start(), calls=%async_computation.11 | async-start | bytes 1966080 | tf_op jit(solution)/shard_map/all_gather | solution.py:681
  1198.7 72.1 %copy-start.32 = (bf16[8,2048,16]{1,2,0:T(8,128)(2,1)S(1)}, bf16[8,2048,16]{1,2,0:T(8,128)(2,1)}, u32[]{:S(2)}) copy-start(bf16[8,2048,16]{1,2,0:T(8,128)(2,1)} %param.48) | copy-start | bytes 1572868
  1198.7 72.1 %copy-start.34 = (bf16[8,2048,16]{1,2,0:T(8,128)(2,1)S(1)}, bf16[8,2048,16]{1,2,0:T(8,128)(2,1)}, u32[]{:S(2)}) copy-start(bf16[8,2048,16]{1,2,0:T(8,128)(2,1)} %param.46) | copy-start | bytes 1572868
  1198.7 72.1 %copy-start.41 = (f32[2048]{0:T(1024)S(1)}, f32[2048]{0:T(1024)}, u32[]{:S(2)}) copy-start(f32[2048]{0:T(1024)} %copy-done.40) | copy-start | bytes 24580
  1270.7 68.3 %all-gather.27.cloned.1.call-start = ((), (), s32[]{:S(2)}) async-start(), calls=%async_computation.12 | async-start | bytes 2621440 | tf_op jit(solution)/shard_map/all_gather | solution.py:681
  1270.8 8.2 slice-start.2
  1270.8 8.2 copy-start.44
  1270.8 8.2 copy-start.4
  1270.8 8.8 slice-start.3
  1279.7 4.4 copy-start.15
  1342.1 7.0 copy-start.1
  (3 other events, 3.7 us)
Sparse Core Ops, SparseCore 0:
  24.6 96.8 all-gather.14
  123.4 124.0 all-gather.16
  249.3 176.2 all-gather.20
  427.3 132.6 all-gather.18
  561.7 131.8 all-gather.22
  855.5 123.6 reduce-scatter.8
  1131.3 67.2 reduce-scatter.6
  1201.1 67.7 all-reduce.4
  1271.4 30.1 all-gather.24
  1303.8 35.1 all-gather.26
